TPU v7x, 256 devices: a whole 4x4x8 slice. The times are simulated.
256 devices in a mesh: row: 8 (over y, x_hi), col: 32 (over x_lo, z, core).
Axes of the slice: x: 4 (x_hi: 2, x_lo: 2; x = x_hi * 2 + x_lo), y: 4, z: 8, core: 2. Of those that a mesh axis runs over, the one named last changes fastest.
Arguments:
- inverse_block: float32 [12288, 12288], P('row', 'col'), may hold values from -6 to 6
- factor_panel: float32 [3, 12288, 256], P(None, ('row', 'col')), may hold values from -0.0546875 to 0.0546875
- diag_inverse: float32 [3, 256, 256], P(None, 'row'), may hold values from -6 to 6
- block_lists: int32 [3, 48], replicated, may hold values from 0 to 47, as said below
- list_counts: int32 [3], replicated, may hold values from 6 to 48, as said below
Outputs:
- solved: float32 [3, 12288, 256], P(None, ('row', 'col'))
- diag_block: float32 [3, 256, 256], P(None, 'row')
Inputs may be any that keep to these rules, and one draw needn't show every extreme that they name: `block_lists`: row k is an ordering of all 48 ancestor blocks; its first list_counts[k] entries are the blocks listed for supernode k. `list_counts`: one supernode lists all 48 blocks and one lists 48 // 8 of them.
All inputs are finite; a program needn't handle non-finite values.
Results may differ from a plain program's by a relative error of at most 0.000071.
Values sent between devices are 32-bit elements; how exact they have to be, the bound alone decides.
No kernel may reach another device: no remote copies, remote signals or barrier semaphores. Data moves between devices by JAX's collectives and lax.ppermute only.
A program may use at most 64 MiB of HBM per device.

v0:
```python
import jax
import jax.numpy as jnp
import numpy as np
from jax import lax
from jax.experimental import pallas as pl
from jax.experimental.pallas import tpu as pltpu
from jax.sharding import PartitionSpec as P


BLK = 256
SEGMENT = 16
VMEM_LIMIT = 20 * 1024 * 1024
DIMS = (4, 2, 2, 8, 2)
AXES = ("row", "col")


def send(array, target):
    pairs = []
    for source in range(int(np.prod(DIMS))):
        place = tuple(int(i) for i in np.unravel_index(source, DIMS))
        pairs.append((source, int(np.ravel_multi_index(target(*place), DIMS))))
    return lax.ppermute(array, AXES, pairs)


def other_core(y, xh, xl, z, c):
    return (y, xh, xl, z, 1 - c)


def other_xl(y, xh, xl, z, c):
    return (y, xh, 1 - xl, z, c)


def other_xh(y, xh, xl, z, c):
    return (y, 1 - xh, xl, z, c)


def ahead(c):
    return 1 - 2 * c


def back(c):
    return 2 * c - 1


def y_by(move):
    return lambda y, xh, xl, z, c: ((y + move(c)) % 4, xh, xl, z, c)


def z_by(move):
    return lambda y, xh, xl, z, c: (y, xh, xl, (z + move(c)) % 8, c)


def y_pair(y, xh, xl, z, c):
    return (y ^ (3 if c else 1), xh, xl, z, c)


def z_pair(bit):
    return lambda y, xh, xl, z, c: (y, xh, xl, (((z + c) % 8 ^ bit) - c) % 8, c)


SHARES = (
    (5, 8, 10, 7, 14, 11, 4, 1, 2, 13, 15, 0, 9, 6, 3, 12),
    (11, 7, 4, 10, 0, 9, 3, 13, 5, 14, 1, 2, 12, 15, 6, 8),
    (1, 8, 11, 0, 7, 4, 12, 10, 6, 3, 9, 14, 2, 5, 15, 13),
    (12, 14, 7, 15, 11, 0, 8, 4, 2, 9, 3, 6, 13, 1, 5, 10),
    (8, 7, 13, 4, 11, 0, 14, 3, 10, 1, 12, 5, 2, 15, 6, 9),
    (1, 4, 14, 9, 3, 13, 2, 12, 5, 0, 8, 11, 6, 7, 15, 10),
    (15, 12, 1, 4, 3, 8, 6, 0, 9, 10, 13, 5, 11, 14, 2, 7),
    (9, 3, 13, 0, 15, 6, 2, 7, 12, 4, 5, 8, 1, 10, 11, 14),
    (14, 1, 12, 5, 2, 6, 13, 11, 8, 4, 9, 3, 15, 0, 10, 7),
    (12, 9, 3, 0, 10, 8, 1, 6, 14, 7, 4, 15, 11, 13, 5, 2),
    (5, 0, 3, 6, 14, 2, 1, 9, 13, 4, 10, 12, 11, 7, 8, 15),
    (8, 5, 13, 0, 2, 11, 7, 15, 12, 1, 4, 10, 3, 6, 14, 9),
    (6, 14, 15, 3, 7, 10, 12, 5, 8, 4, 2, 9, 0, 13, 1, 11),
    (1, 2, 9, 10, 4, 15, 11, 8, 7, 3, 14, 13, 12, 6, 5, 0),
    (9, 11, 3, 6, 13, 8, 10, 15, 2, 14, 7, 1, 0, 5, 4, 12),
    (3, 10, 7, 15, 0, 13, 4, 9, 14, 11, 1, 6, 8, 5, 2, 12),
)


def column_target():
    target = {}
    for column, shares in enumerate(SHARES):
        xl, z = column // 8, column % 8
        for slot, share in enumerate(shares):
            source = (xl * 2 + z // 4, z // 2 % 2, z % 2, share // 2, share % 2)
            target[source] = (slot // 4, slot // 2 % 2, xl, z, slot % 2)
    return target


COLUMN_TARGET = column_target()


def to_column(*place):
    return COLUMN_TARGET[place]


def listed_blocks(block_lists, list_counts, blocks):
    entries = jnp.arange(block_lists.shape[1], dtype=jnp.int32)
    active = entries[None, :] < list_counts[:, None]
    hits = (block_lists[:, None, :] == blocks[None, :, None]) & active[:, None, :]
    return jnp.any(hits, axis=2)


def pick(array, index, axis):
    return lax.dynamic_index_in_dim(array, index, axis, keepdims=False)


def place_of(row, col):
    return row // 2, row % 2, col // 16, col // 2 % 8, col % 2


def split(value):
    high = lax.reduce_precision(value, 8, 7)
    return high.astype(jnp.bfloat16), (value - high).astype(jnp.bfloat16)


def split_value(value):
    high = value.astype(jnp.bfloat16)
    return high, (value - high.astype(jnp.float32)).astype(jnp.bfloat16)


def multiply_kernel(share_ref, listed_ref, left_high, left_low, *refs):
    pieces, (out, opposite, right_high, right_low) = refs[:8], refs[8:]
    nsn, rows, width = pieces[0].shape[0] // 2, pieces[0].shape[1], pieces[0].shape[2]
    depth = right_high.shape[0]
    y, xh, xl, z, core = place_of(lax.axis_index("row"), lax.axis_index("col"))
    column = xl * 8 + z
    for j, piece in enumerate(pieces):
        dy, c = j % 4, (core if j < 4 else 1 - core)
        for dxh in range(2):
            slot = ((y + 4 + (1 - 2 * c) * dy) % 4 * 2 + (xh + dxh) % 2) * 2 + c
            start = share_ref[column * 16 + slot] * rows
            for part in range(0, rows, SEGMENT):
                place = pl.multiple_of(start + part, SEGMENT)
                block = column * (depth // BLK) + place // BLK
                for k in range(nsn):
                    flag = listed_ref[k, block].astype(jnp.float32)
                    high, low = split_value(piece[dxh * nsn + k, part : part + SEGMENT] * flag)
                    lanes = slice(k * width, (k + 1) * width)
                    right_high[pl.ds(place, SEGMENT), lanes] = high
                    right_low[pl.ds(place, SEGMENT), lanes] = low

    def dot(left, right):
        return jnp.dot(left, right, preferred_element_type=jnp.float32)

    for i in range(0, out.shape[0], BLK):
        band = slice(i, i + BLK)
        out[band, :] = (
            dot(left_high[band, :], right_high[...])
            + dot(left_high[band, :], right_low[...])
            + dot(left_low[band, :], right_high[...])
        )
    for x in range(2):
        opposite[x] = out[pl.ds(pl.multiple_of((x * 8 + (z + 4) % 8) * rows, SEGMENT), rows), :]


def multiply(listed, left_high, left_low, pieces):
    size, depth = left_high.shape
    rows = pieces[0].shape[1]
    wide = pieces[0].shape[0] // 2 * pieces[0].shape[2]
    whole = pl.BlockSpec(memory_space=pltpu.VMEM)
    scalars = pl.BlockSpec(memory_space=pltpu.SMEM)
    return pl.pallas_call(
        multiply_kernel,
        out_shape=[
            jax.ShapeDtypeStruct((size, wide), jnp.float32),
            jax.ShapeDtypeStruct((2, rows, wide), jnp.float32),
        ],
        in_specs=[scalars, scalars] + [whole] * (2 + len(pieces)),
        out_specs=[whole, whole],
        scratch_shapes=[pltpu.VMEM((depth, wide), jnp.bfloat16)] * 2,
        compiler_params=pltpu.CompilerParams(vmem_limit_bytes=VMEM_LIMIT),
        cost_estimate=pl.CostEstimate(flops=6 * size * wide * depth, bytes_accessed=12 * size * wide, transcendentals=0),
        name="multiply",
    )(jnp.asarray(np.array(SHARES, np.int32).reshape(-1)), listed, left_high, left_low, *pieces)


def terms_kernel(listed_ref, product, *refs):
    parts, (keep, give, left_high, left_low, right_high, right_low) = refs[:8], refs[8:]
    nsn, rows, width = parts[0].shape[0] // 2, parts[0].shape[1], parts[0].shape[2]
    row, col = lax.axis_index("row"), lax.axis_index("col")
    _, _, _, z, core = place_of(row, col)
    for d, part in enumerate(parts):
        chip = (z + 8 + (1 - 2 * core) * d) % 8
        for x in range(2):
            here = slice((d * 2 + x) * rows, (d * 2 + x + 1) * rows)
            value = product[pl.ds(pl.multiple_of((x * 8 + chip) * rows, SEGMENT), rows), :]
            right_high[here, :], right_low[here, :] = split_value(value)
            first = (row * 32 + x * 16 + chip * 2 + core) * rows
            for s in range(0, rows, SEGMENT):
                for k in range(nsn):
                    flag = listed_ref[k, (first + s) // BLK].astype(jnp.float32)
                    high, low = split_value(part[x * nsn + k, s : s + SEGMENT] * flag)
                    spot = (slice(here.start + s, here.start + s + SEGMENT), slice(k * width, (k + 1) * width))
                    left_high[spot], left_low[spot] = high, low

    def dot(left, right, lanes):
        return lax.dot_general(
            left[:, lanes], right[:, lanes], (((0,), (0,)), ((), ())), preferred_element_type=jnp.float32
        )

    for k in range(nsn):
        lanes = slice(k * width, (k + 1) * width)
        value = (
            dot(left_high, right_high, lanes) + dot(left_high, right_low, lanes) + dot(left_low, right_high, lanes)
        )
        below, above = value[:, : width // 2], value[:, width // 2 :]
        keep[k] = jnp.where(core == 0, below, above)
        give[k] = jnp.where(core == 0, above, below)


def diagonal_terms(listed, product, parts):
    size, wide = product.shape
    nsn, width = parts[0].shape[0] // 2, parts[0].shape[2]
    whole = pl.BlockSpec(memory_space=pltpu.VMEM)
    return pl.pallas_call(
        terms_kernel,
        out_shape=[jax.ShapeDtypeStruct((nsn, width, width // 2), jnp.float32)] * 2,
        in_specs=[pl.BlockSpec(memory_space=pltpu.SMEM)] + [whole] * (1 + len(parts)),
        out_specs=[whole, whole],
        scratch_shapes=[pltpu.VMEM((size, wide), jnp.bfloat16)] * 4,
        compiler_params=pltpu.CompilerParams(vmem_limit_bytes=VMEM_LIMIT),
        cost_estimate=pl.CostEstimate(
            flops=6 * size * wide * width, bytes_accessed=8 * size * wide, transcendentals=0
        ),
        name="terms",
    )(listed, product, *parts)


def both(*arrays):
    return lax.optimization_barrier(arrays)


def per_device(inverse_block, factor_panel, diag_inverse, block_lists, list_counts):
    row, col = lax.axis_index("row"), lax.axis_index("col")
    y, xh, xl, z, core = place_of(row, col)
    nsn, rows, width = factor_panel.shape
    span = inverse_block.shape[1]

    def facing(array):
        return send(array, other_core)

    share = send(factor_panel, to_column)
    beside = send(factor_panel, other_xl)
    after, beside = both(core, beside)
    halves = inverse_block.reshape(16, 2, rows, span)
    s_own = pick(halves, after, 1).reshape(16 * rows, span)
    s_other = facing(pick(halves, 1 - after, 1).reshape(16 * rows, span))
    share, beside, s_other = both(share, beside, s_other)

    near = send(share, other_xh)
    line = jnp.concatenate(
        [jnp.where(xl == 0, factor_panel, beside), jnp.where(xl == 0, beside, factor_panel)]
    )
    line_from1, line_to1 = send(line, z_by(ahead)), send(line, z_by(back))
    s_chip = jnp.concatenate(
        [jnp.where(core == 0, s_own, s_other), jnp.where(core == 0, s_other, s_own)], axis=1
    )
    s_high, s_low = split(s_chip)
    listed = listed_blocks(block_lists, list_counts, jnp.arange(block_lists.shape[1], dtype=jnp.int32))
    listed = listed.astype(jnp.int32)
    near, line_from1, line_to1, s_high, s_low, listed = both(near, line_from1, line_to1, s_high, s_low, listed)

    pair = jnp.concatenate([share, near])
    from1, to1 = send(pair, y_by(ahead)), send(pair, y_by(back))
    line_from2, line_to2 = send(line_from1, z_by(ahead)), send(line_to1, z_by(back))
    pair_facing = facing(pair)
    from1, to1, line_from2, line_to2, pair_facing = both(from1, to1, line_from2, line_to2, pair_facing)

    far = send(from1, y_by(ahead))
    line_from3, line_to3 = send(line_from2, z_by(ahead)), send(line_to2, z_by(back))
    from1_facing, to1_facing = facing(from1), facing(to1)
    far, line_from3, line_to3, from1_facing, to1_facing = both(far, line_from3, line_to3, from1_facing, to1_facing)
    line_far = send(line_from3, z_by(ahead))
    pieces = [pair, to1, far, from1, pair_facing, to1_facing, facing(far), from1_facing]
    product, opposite = multiply(listed, s_high, s_low, pieces)
    stacked = product.reshape(2, 8, rows, nsn * width)

    def at(distance):
        return pick(stacked, (z + (1 - 2 * core) * distance) % 8, 1)

    opposite = send(opposite, z_by(ahead))
    first, second = send(at(3) + opposite, z_by(ahead)), send(at(-3), z_by(back))
    first, second = send(at(2) + first, z_by(ahead)), send(at(-2) + second, z_by(back))
    first, second = send(at(1) + first, z_by(ahead)), send(at(-1) + second, z_by(back))
    partial = at(0) + first + second
    crossed = send(pick(partial, 1 - xl, 0), other_xl)
    total = pick(partial, xl, 0) + crossed
    row_blocks = ((row * 32 + col) * rows + jnp.arange(rows, dtype=jnp.int32)) // BLK
    mask = listed_blocks(block_lists, list_counts, row_blocks).astype(jnp.float32)
    solved = jnp.stack([total[:, k * width : (k + 1) * width] for k in range(nsn)])
    solved = -solved * mask[:, :, None]

    keep, give = diagonal_terms(
        listed, product, [line, line_to1, line_to2, line_to3, line_far, line_from3, line_from2, line_from1]
    )
    terms = (keep + facing(give)).reshape(nsn, 2, 2, 2, width // 8, width // 2)
    terms = pick(terms, y % 2, 2) + send(pick(terms, 1 - y % 2, 2), y_pair)
    terms = pick(terms, y // 2, 1) + send(pick(terms, 1 - y // 2, 1), y_by(lambda c: 2))
    terms = pick(terms, xh, 1) + send(pick(terms, 1 - xh, 1), other_xh)
    terms = terms + send(terms, other_xl)
    terms = terms + send(terms, z_pair(1))
    terms = terms + send(terms, z_pair(2))
    terms = terms + send(terms, z_pair(4))
    rest = facing(terms)
    diag_block = diag_inverse + jnp.concatenate(
        [jnp.where(core == 0, terms, rest), jnp.where(core == 0, rest, terms)], axis=2
    )
    return (solved, diag_block)


def solution(mesh):
    placed = (P("row", "col"), P(None, ("row", "col"), None), P(None, "row", None), P(), P())
    return jax.shard_map(
        per_device,
        mesh=mesh,
        in_specs=placed,
        out_specs=(P(None, ("row", "col"), None), P(None, "row", None)),
        check_vma=False,
    )
```

profile of v0, /device:TPU:6, one launch (start us, length us, event | category | flops | bytes accessed | tf_op | source)
XLA Modules:
  0.0 143.3 jit_solution(12693677771908621358)
XLA Ops:
  1.5 5.0 %collective-permute-done.1 = f32[3,48,256]{2,1,0:T(8,128)S(1)} collective-permute-done((f32[3,48,256]{2,1,0:T(8,128)}, f32[3,48,256]{2,1,0:T(8,128)S(1)}, u32[]{:S(2)}, u32[]{:S(2)}) %collective-permute-start.1) | collective-permute-done | bytes 147488 | tf_op jit(solution)/shard_map/ppermute | solution.py:22
  7.2 1.8 %constant_dynamic-slice_fusion.2 = (f32[16,1,48,384]{3,2,1,0:T(8,128)S(1)}, f32[16,1,48,384]{3,2,1,0:T(8,128)S(1)}) fusion(f32[16,2,48,384]{3,2,1,0:T(8,128)} %bitcast.70, s32[]{:T(128)S(6)} %select_n.172, s32[]{:T(128)S(6)} %select_n.166), kind=kLoop, calls=%fused_computation.41 | loop fusion | bytes 4718600 | tf_op jit(solution)/shard_map/jit(dynamic_index_in_dim)/dynamic_slice | solution.py:106
  9.1 5.7 %collective-permute-start = (f32[3,48,256]{2,1,0:T(8,128)}, f32[3,48,256]{2,1,0:T(8,128)}, u32[]{:S(2)}, u32[]{:S(2)}) collective-permute-start(f32[3,48,256]{2,1,0:T(8,128)} %param.7), channel_id=1, source_target_pairs={{0,161},{1,97},{2,128},{3,224},{4,96},{5,0},{6,193},{7,33},{8,1},{... | collective-permute-start | bytes 442376 | tf_op jit(solution)/shard_map/ppermute | solution.py:22
  15.1 16.8 %collective-permute-done = f32[3,48,256]{2,1,0:T(8,128)} collective-permute-done((f32[3,48,256]{2,1,0:T(8,128)}, f32[3,48,256]{2,1,0:T(8,128)}, u32[]{:S(2)}, u32[]{:S(2)}) %collective-permute-start) | collective-permute-done | bytes 147488 | tf_op jit(solution)/shard_map/ppermute | solution.py:22
  33.1 3.2 %collective-permute-start.5 = (f32[6,48,256]{2,1,0:T(8,128)S(1)}, f32[6,48,256]{2,1,0:T(8,128)S(1)}, u32[]{:S(2)}, u32[]{:S(2)}) collective-permute-start(f32[6,48,256]{2,1,0:T(8,128)S(1)} %pad_maximum_fusion.1.refs_0_), channel_id=1, source_target_pairs={{0,14},{1,3},{2,0},{3,5},{4,2},{5,7},{6,4},{7,9},{8,6},{9,11},{10,... | collective-permute-start | bytes 884744 | tf_op jit(solution)/shard_map/ppermute | solution.py:22
  36.3 1.3 collective-permute-start.3
  39.1 4.1 %collective-permute-done.3 = f32[3,48,256]{2,1,0:T(8,128)S(1)} collective-permute-done((f32[3,48,256]{2,1,0:T(8,128)}, f32[3,48,256]{2,1,0:T(8,128)S(1)}, u32[]{:S(2)}, u32[]{:S(2)}) %collective-permute-start.3) | collective-permute-done | bytes 147488 | tf_op jit(solution)/shard_map/ppermute | solution.py:22
  44.3 3.2 %collective-permute-start.7 = (f32[6,48,256]{2,1,0:T(8,128)S(1)}, f32[6,48,256]{2,1,0:T(8,128)S(1)}, u32[]{:S(2)}, u32[]{:S(2)}) collective-permute-start(f32[6,48,256]{2,1,0:T(8,128)S(1)} %constant_dynamic-update-slice_fusion.refs_0_), channel_id=1, source_target_pairs={{0,192},{1,65},{2,194},{3,67},{4,196},{5,69},{6,198},{7,71},{8,200... | collective-permute-start | bytes 884744 | tf_op jit(solution)/shard_map/ppermute | solution.py:22
  47.6 3.2 %collective-permute-start.9 = (f32[6,48,256]{2,1,0:T(8,128)S(1)}, f32[6,48,256]{2,1,0:T(8,128)S(1)}, u32[]{:S(2)}, u32[]{:S(2)}) collective-permute-start(f32[6,48,256]{2,1,0:T(8,128)S(1)} %collective-permute-done.5.refs_1_), channel_id=1, source_target_pairs={{0,14},{1,3},{2,0},{3,5},{4,2},{5,7},{6,4},{7,9},{8,6},{9,11},{10,... | collective-permute-start | bytes 884744 | tf_op jit(solution)/shard_map/ppermute | solution.py:22
  50.8 4.1 %collective-permute-done.6.refs_3_ = f32[6,48,256]{2,1,0:T(8,128)S(1)} collective-permute-done((f32[6,48,256]{2,1,0:T(8,128)S(1)}, f32[6,48,256]{2,1,0:T(8,128)S(1)}, u32[]{:S(2)}, u32[]{:S(2)}) %collective-permute-start.6) | collective-permute-done | bytes 294944 | tf_op jit(solution)/shard_map/ppermute | solution.py:22
  54.9 2.0 %collective-permute-done.8.refs_6_ = f32[6,48,256]{2,1,0:T(8,128)S(1)} collective-permute-done((f32[6,48,256]{2,1,0:T(8,128)S(1)}, f32[6,48,256]{2,1,0:T(8,128)S(1)}, u32[]{:S(2)}, u32[]{:S(2)}) %collective-permute-start.8) | collective-permute-done | bytes 294944 | tf_op jit(solution)/shard_map/ppermute | solution.py:22
  57.0 3.2 %collective-permute-start.13 = (f32[6,48,256]{2,1,0:T(8,128)S(1)}, f32[6,48,256]{2,1,0:T(8,128)S(1)}, u32[]{:S(2)}, u32[]{:S(2)}) collective-permute-start(f32[6,48,256]{2,1,0:T(8,128)S(1)} %collective-permute-done.9.refs_2_), channel_id=1, source_target_pairs={{0,14},{1,3},{2,0},{3,5},{4,2},{5,7},{6,4},{7,9},{8,6},{9,11},{10,... | collective-permute-start | bytes 884744 | tf_op jit(solution)/shard_map/ppermute | solution.py:22
  60.2 4.6 %collective-permute-done.11.refs_2_ = f32[6,48,256]{2,1,0:T(8,128)S(1)} collective-permute-done((f32[6,48,256]{2,1,0:T(8,128)S(1)}, f32[6,48,256]{2,1,0:T(8,128)S(1)}, u32[]{:S(2)}, u32[]{:S(2)}) %collective-permute-start.11) | collective-permute-done | bytes 294944 | tf_op jit(solution)/shard_map/ppermute | solution.py:22
  64.8 2.1 %collective-permute-done.12.refs_5_ = f32[6,48,256]{2,1,0:T(8,128)S(1)} collective-permute-done((f32[6,48,256]{2,1,0:T(8,128)S(1)}, f32[6,48,256]{2,1,0:T(8,128)S(1)}, u32[]{:S(2)}, u32[]{:S(2)}) %collective-permute-start.12) | collective-permute-done | bytes 294944 | tf_op jit(solution)/shard_map/ppermute | solution.py:22
  69.1 4.2 %multiply.1 = (f32[768,768]{1,0:T(8,128)S(1)}, f32[2,48,768]{2,1,0:T(8,128)S(1)}) custom-call(s32[256]{0:T(256)S(1)} %copy-done, s32[3,48]{1,0:T(4,128)S(1)} %convert_element_type.18.listed_ref, bf16[768,768]{1,0:T(8,128)(2,1)S(1)} %get-tuple-element.33.left_high, bf16[768,768]{1,0:T(8,128)(2,1)S(1)} %get-tuple-element.34.left_low, ...), custom_call_target="tpu_custom_call" | custom-call | flops 2717908992 | bytes 7077888 | tf_op jit(solution)/shard_map/multiply/pallas_call | solution.py:164
  73.2 2.5 %collective-permute-done.25.refs_4_ = f32[6,48,256]{2,1,0:T(8,128)S(1)} collective-permute-done((f32[6,48,256]{2,1,0:T(8,128)S(1)}, f32[6,48,256]{2,1,0:T(8,128)S(1)}, u32[]{:S(2)}, u32[]{:S(2)}) %collective-permute-start.25) | collective-permute-done | bytes 294944 | tf_op jit(solution)/shard_map/ppermute | solution.py:22
  75.8 2.1 %terms.1 = (f32[3,256,128]{2,1,0:T(8,128)S(1)}, f32[3,256,128]{2,1,0:T(8,128)S(1)}) custom-call(s32[3,48]{1,0:T(4,128)S(1)} %convert_element_type.18.listed_ref, f32[768,768]{1,0:T(8,128)S(1)} %get-tuple-element.46.product, f32[6,48,256]{2,1,0:T(8,128)S(1)} %pad_maximum_fusion.1.refs_0_, f32[6,48,256]{2,1,0:T(8,128)S(1)} %collective-permute-done.5.refs_1_, ...), custom_call_target="tpu_custom_call" | custom-call | flops 905969664 | bytes 4718592 | tf_op jit(solution)/shard_map/terms/pallas_call | solution.py:217
  78.3 3.1 %collective-permute-start.21 = (f32[2,48,768]{2,1,0:T(8,128)S(1)}, f32[2,48,768]{2,1,0:T(8,128)S(1)}, u32[]{:S(2)}, u32[]{:S(2)}) collective-permute-start(f32[2,48,768]{2,1,0:T(8,128)S(1)} %dynamic-slice_bitcast_fusion), channel_id=1, source_target_pairs={{0,14},{1,3},{2,0},{3,5},{4,2},{5,7},{6,4},{7,9},{8,6},{9,11},{10,... | collective-permute-start | bytes 884744 | tf_op jit(solution)/shard_map/ppermute | solution.py:22
  83.0 6.1 %collective-permute-done.17 = f32[2,48,768]{2,1,0:T(8,128)} collective-permute-done((f32[2,48,768]{2,1,0:T(8,128)S(1)}, f32[2,48,768]{2,1,0:T(8,128)}, u32[]{:S(2)}, u32[]{:S(2)}) %collective-permute-start.17) | collective-permute-done | bytes 294944 | tf_op jit(solution)/shard_map/ppermute | solution.py:22
  90.3 2.6 %collective-permute-start.28 = (f32[3,2,32,128]{3,2,0,1:T(8,128)S(1)}, f32[3,2,32,128]{3,2,0,1:T(8,128)S(1)}, u32[]{:S(2)}, u32[]{:S(2)}) collective-permute-start(f32[3,2,32,128]{3,2,0,1:T(8,128)S(1)} %bitcast.74), channel_id=1, source_target_pairs={{0,128},{1,129},{2,130},{3,131},{4,132},{5,133},{6,134},{7,135},{8... | collective-permute-start | bytes 294920 | tf_op jit(solution)/shard_map/ppermute | solution.py:22
  92.8 5.2 %collective-permute-done.18 = f32[2,48,768]{2,1,0:T(8,128)S(1)} collective-permute-done((f32[2,48,768]{2,1,0:T(8,128)S(1)}, f32[2,48,768]{2,1,0:T(8,128)S(1)}, u32[]{:S(2)}, u32[]{:S(2)}) %collective-permute-start.18) | collective-permute-done | bytes 294944 | tf_op jit(solution)/shard_map/ppermute | solution.py:22
  98.3 3.2 %collective-permute-start.29 = (f32[3,32,128]{2,1,0:T(8,128)S(1)}, f32[3,32,128]{2,1,0:T(8,128)S(1)}, u32[]{:S(2)}, u32[]{:S(2)}) collective-permute-start(f32[3,32,128]{2,1,0:T(8,128)S(1)} %dynamic-slice_bitcast_fusion.3), channel_id=1, source_target_pairs={{0,32},{1,33},{2,34},{3,35},{4,36},{5,37},{6,38},{7,39},{8,40},{9,... | collective-permute-start | bytes 147464 | tf_op jit(solution)/shard_map/ppermute | solution.py:22
  101.5 7.8 %collective-permute-done.19 = f32[2,48,768]{2,1,0:T(8,128)S(1)} collective-permute-done((f32[2,48,768]{2,1,0:T(8,128)S(1)}, f32[2,48,768]{2,1,0:T(8,128)S(1)}, u32[]{:S(2)}, u32[]{:S(2)}) %collective-permute-start.19) | collective-permute-done | bytes 294944 | tf_op jit(solution)/shard_map/ppermute | solution.py:22
  109.8 4.1 %collective-permute-done.30 = f32[3,32,128]{2,1,0:T(8,128)S(1)} collective-permute-done((f32[3,32,128]{2,1,0:T(8,128)S(1)}, f32[3,32,128]{2,1,0:T(8,128)S(1)}, u32[]{:S(2)}, u32[]{:S(2)}) %collective-permute-start.30) | collective-permute-done | bytes 49184 | tf_op jit(solution)/shard_map/ppermute | solution.py:22
  113.9 2.1 %collective-permute-start.31 = (f32[3,32,128]{2,1,0:T(8,128)S(1)}, f32[3,32,128]{2,1,0:T(8,128)S(1)}, u32[]{:S(2)}, u32[]{:S(2)}) collective-permute-start(f32[3,32,128]{2,1,0:T(8,128)S(1)} %add.237), channel_id=1, source_target_pairs={{0,2},{1,15},{2,0},{3,5},{4,6},{5,3},{6,4},{7,9},{8,10},{9,7},{10,... | collective-permute-start | bytes 147464 | tf_op jit(solution)/shard_map/ppermute | solution.py:22
  116.0 2.1 %collective-permute-done.31 = f32[3,32,128]{2,1,0:T(8,128)S(1)} collective-permute-done((f32[3,32,128]{2,1,0:T(8,128)S(1)}, f32[3,32,128]{2,1,0:T(8,128)S(1)}, u32[]{:S(2)}, u32[]{:S(2)}) %collective-permute-start.31) | collective-permute-done | bytes 49184 | tf_op jit(solution)/shard_map/ppermute | solution.py:22
  118.2 5.5 %collective-permute-done.32 = f32[3,32,128]{2,1,0:T(8,128)S(1)} collective-permute-done((f32[3,32,128]{2,1,0:T(8,128)S(1)}, f32[3,32,128]{2,1,0:T(8,128)S(1)}, u32[]{:S(2)}, u32[]{:S(2)}) %collective-permute-start.32) | collective-permute-done | bytes 49184 | tf_op jit(solution)/shard_map/ppermute | solution.py:22
  123.7 3.9 %collective-permute-start.33 = (f32[3,32,128]{2,1,0:T(8,128)S(1)}, f32[3,32,128]{2,1,0:T(8,128)S(1)}, u32[]{:S(2)}, u32[]{:S(2)}) collective-permute-start(f32[3,32,128]{2,1,0:T(8,128)S(1)} %add.239), channel_id=1, source_target_pairs={{0,8},{1,9},{2,10},{3,11},{4,12},{5,13},{6,14},{7,15},{8,0},{9,1},... | collective-permute-start | bytes 147464 | tf_op jit(solution)/shard_map/ppermute | solution.py:22
  127.6 2.1 %collective-permute-start.20 = (f32[2,48,768]{2,1,0:T(8,128)S(1)}, f32[2,48,768]{2,1,0:T(8,128)S(1)}, u32[]{:S(2)}, u32[]{:S(2)}) collective-permute-start(f32[2,48,768]{2,1,0:T(8,128)S(1)} %get-tuple-element.54), channel_id=1, source_target_pairs={{0,2},{1,15},{2,4},{3,1},{4,6},{5,3},{6,8},{7,5},{8,10},{9,7},{10,... | collective-permute-start | bytes 884744 | tf_op jit(solution)/shard_map/ppermute | solution.py:22
  132.5 1.6 %collective-permute-done.34 = f32[3,32,128]{2,1,0:T(8,128)} collective-permute-done((f32[3,32,128]{2,1,0:T(8,128)}, f32[3,32,128]{2,1,0:T(8,128)}, u32[]{:S(2)}, u32[]{:S(2)}) %collective-permute-start.34) | collective-permute-done | bytes 49184 | tf_op jit(solution)/shard_map/ppermute | solution.py:22
  136.6 2.8 %collective-permute-start.24 = (f32[48,768]{1,0:T(8,128)S(1)}, f32[48,768]{1,0:T(8,128)S(1)}, u32[]{:S(2)}, u32[]{:S(2)}) collective-permute-start(f32[48,768]{1,0:T(8,128)S(1)} %dynamic-slice_bitcast_fusion.2), channel_id=1, source_target_pairs={{0,16},{1,17},{2,18},{3,19},{4,20},{5,21},{6,22},{7,23},{8,24},{9,... | collective-permute-start | bytes 442376 | tf_op jit(solution)/shard_map/ppermute | solution.py:22
  140.1 2.5 %collective-permute-done.24 = f32[48,768]{1,0:T(8,128)S(1)} collective-permute-done((f32[48,768]{1,0:T(8,128)S(1)}, f32[48,768]{1,0:T(8,128)S(1)}, u32[]{:S(2)}, u32[]{:S(2)}) %collective-permute-start.24) | collective-permute-done | bytes 147488 | tf_op jit(solution)/shard_map/ppermute | solution.py:22
  (86 shorter events, 18.6 us)
Async XLA Ops:
  0.6 5.9 %collective-permute-start.1 = (f32[3,48,256]{2,1,0:T(8,128)}, f32[3,48,256]{2,1,0:T(8,128)S(1)}, u32[]{:S(2)}, u32[]{:S(2)}) collective-permute-start(f32[3,48,256]{2,1,0:T(8,128)} %param.7), channel_id=1, source_target_pairs={{0,16},{1,17},{2,18},{3,19},{4,20},{5,21},{6,22},{7,23},{8,24},{9,... | collective-permute-start | bytes 442376 | tf_op jit(solution)/shard_map/ppermute | solution.py:22
  9.0 23.0 %collective-permute-start.2 = (f32[768,384]{1,0:T(8,128)S(1)}, f32[768,384]{1,0:T(8,128)S(1)}, u32[]{:S(2)}, u32[]{:S(2)}) collective-permute-start(f32[768,384]{1,0:T(8,128)S(1)} %bitcast.73), channel_id=1, source_target_pairs={{0,1},{1,0},{2,3},{3,2},{4,5},{5,4},{6,7},{7,6},{8,9},{9,8},{10,11... | collective-permute-start | bytes 3538952 | tf_op jit(solution)/shard_map/ppermute | solution.py:22
  9.1 22.9 %collective-permute-start = (f32[3,48,256]{2,1,0:T(8,128)}, f32[3,48,256]{2,1,0:T(8,128)}, u32[]{:S(2)}, u32[]{:S(2)}) collective-permute-start(f32[3,48,256]{2,1,0:T(8,128)} %param.7), channel_id=1, source_target_pairs={{0,161},{1,97},{2,128},{3,224},{4,96},{5,0},{6,193},{7,33},{8,1},{... | collective-permute-start | bytes 442376 | tf_op jit(solution)/shard_map/ppermute | solution.py:22
  33.0 11.1 %collective-permute-start.4 = (f32[6,48,256]{2,1,0:T(8,128)S(1)}, f32[6,48,256]{2,1,0:T(8,128)S(1)}, u32[]{:S(2)}, u32[]{:S(2)}) collective-permute-start(f32[6,48,256]{2,1,0:T(8,128)S(1)} %pad_maximum_fusion.1.refs_0_), channel_id=1, source_target_pairs={{0,2},{1,15},{2,4},{3,1},{4,6},{5,3},{6,8},{7,5},{8,10},{9,7},{10,... | collective-permute-start | bytes 884744 | tf_op jit(solution)/shard_map/ppermute | solution.py:22
  33.1 11.0 %collective-permute-start.5 = (f32[6,48,256]{2,1,0:T(8,128)S(1)}, f32[6,48,256]{2,1,0:T(8,128)S(1)}, u32[]{:S(2)}, u32[]{:S(2)}) collective-permute-start(f32[6,48,256]{2,1,0:T(8,128)S(1)} %pad_maximum_fusion.1.refs_0_), channel_id=1, source_target_pairs={{0,14},{1,3},{2,0},{3,5},{4,2},{5,7},{6,4},{7,9},{8,6},{9,11},{10,... | collective-permute-start | bytes 884744 | tf_op jit(solution)/shard_map/ppermute | solution.py:22
  36.3 6.9 %collective-permute-start.3 = (f32[3,48,256]{2,1,0:T(8,128)}, f32[3,48,256]{2,1,0:T(8,128)S(1)}, u32[]{:S(2)}, u32[]{:S(2)}) collective-permute-start(f32[3,48,256]{2,1,0:T(8,128)} %collective-permute-done), channel_id=1, source_target_pairs={{0,32},{1,33},{2,34},{3,35},{4,36},{5,37},{6,38},{7,39},{8,40},{9,... | collective-permute-start | bytes 442376 | tf_op jit(solution)/shard_map/ppermute | solution.py:22
  44.1 6.7 %collective-permute-start.10 = (f32[6,48,256]{2,1,0:T(8,128)S(1)}, f32[6,48,256]{2,1,0:T(8,128)S(1)}, u32[]{:S(2)}, u32[]{:S(2)}) collective-permute-start(f32[6,48,256]{2,1,0:T(8,128)S(1)} %constant_dynamic-update-slice_fusion.refs_0_), channel_id=1, source_target_pairs={{0,1},{1,0},{2,3},{3,2},{4,5},{5,4},{6,7},{7,6},{8,9},{9,8},{10,11... | collective-permute-start | bytes 884744 | tf_op jit(solution)/shard_map/ppermute | solution.py:22
  44.3 10.6 %collective-permute-start.6 = (f32[6,48,256]{2,1,0:T(8,128)S(1)}, f32[6,48,256]{2,1,0:T(8,128)S(1)}, u32[]{:S(2)}, u32[]{:S(2)}) collective-permute-start(f32[6,48,256]{2,1,0:T(8,128)S(1)} %constant_dynamic-update-slice_fusion.refs_0_), channel_id=1, source_target_pairs={{0,64},{1,193},{2,66},{3,195},{4,68},{5,197},{6,70},{7,199},{8,72}... | collective-permute-start | bytes 884744 | tf_op jit(solution)/shard_map/ppermute | solution.py:22
  44.3 10.5 %collective-permute-start.7 = (f32[6,48,256]{2,1,0:T(8,128)S(1)}, f32[6,48,256]{2,1,0:T(8,128)S(1)}, u32[]{:S(2)}, u32[]{:S(2)}) collective-permute-start(f32[6,48,256]{2,1,0:T(8,128)S(1)} %constant_dynamic-update-slice_fusion.refs_0_), channel_id=1, source_target_pairs={{0,192},{1,65},{2,194},{3,67},{4,196},{5,69},{6,198},{7,71},{8,200... | collective-permute-start | bytes 884744 | tf_op jit(solution)/shard_map/ppermute | solution.py:22
  47.6 9.3 %collective-permute-start.8 = (f32[6,48,256]{2,1,0:T(8,128)S(1)}, f32[6,48,256]{2,1,0:T(8,128)S(1)}, u32[]{:S(2)}, u32[]{:S(2)}) collective-permute-start(f32[6,48,256]{2,1,0:T(8,128)S(1)} %collective-permute-done.4.refs_7_), channel_id=1, source_target_pairs={{0,2},{1,15},{2,4},{3,1},{4,6},{5,3},{6,8},{7,5},{8,10},{9,7},{10,... | collective-permute-start | bytes 884744 | tf_op jit(solution)/shard_map/ppermute | solution.py:22
  47.6 9.3 %collective-permute-start.9 = (f32[6,48,256]{2,1,0:T(8,128)S(1)}, f32[6,48,256]{2,1,0:T(8,128)S(1)}, u32[]{:S(2)}, u32[]{:S(2)}) collective-permute-start(f32[6,48,256]{2,1,0:T(8,128)S(1)} %collective-permute-done.5.refs_1_), channel_id=1, source_target_pairs={{0,14},{1,3},{2,0},{3,5},{4,2},{5,7},{6,4},{7,9},{8,6},{9,11},{10,... | collective-permute-start | bytes 884744 | tf_op jit(solution)/shard_map/ppermute | solution.py:22
  56.8 7.9 %collective-permute-start.11 = (f32[6,48,256]{2,1,0:T(8,128)S(1)}, f32[6,48,256]{2,1,0:T(8,128)S(1)}, u32[]{:S(2)}, u32[]{:S(2)}) collective-permute-start(f32[6,48,256]{2,1,0:T(8,128)S(1)} %collective-permute-done.6.refs_3_), channel_id=1, source_target_pairs={{0,64},{1,193},{2,66},{3,195},{4,68},{5,197},{6,70},{7,199},{8,72}... | collective-permute-start | bytes 884744 | tf_op jit(solution)/shard_map/ppermute | solution.py:22
  56.8 10.0 %collective-permute-start.14 = (f32[6,48,256]{2,1,0:T(8,128)S(1)}, f32[6,48,256]{2,1,0:T(8,128)S(1)}, u32[]{:S(2)}, u32[]{:S(2)}) collective-permute-start(f32[6,48,256]{2,1,0:T(8,128)S(1)} %collective-permute-done.6.refs_3_), channel_id=1, source_target_pairs={{0,1},{1,0},{2,3},{3,2},{4,5},{5,4},{6,7},{7,6},{8,9},{9,8},{10,11... | collective-permute-start | bytes 884744 | tf_op jit(solution)/shard_map/ppermute | solution.py:22
  56.9 9.9 %collective-permute-start.12 = (f32[6,48,256]{2,1,0:T(8,128)S(1)}, f32[6,48,256]{2,1,0:T(8,128)S(1)}, u32[]{:S(2)}, u32[]{:S(2)}) collective-permute-start(f32[6,48,256]{2,1,0:T(8,128)S(1)} %collective-permute-done.8.refs_6_), channel_id=1, source_target_pairs={{0,2},{1,15},{2,4},{3,1},{4,6},{5,3},{6,8},{7,5},{8,10},{9,7},{10,... | collective-permute-start | bytes 884744 | tf_op jit(solution)/shard_map/ppermute | solution.py:22
  57.0 9.8 %collective-permute-start.13 = (f32[6,48,256]{2,1,0:T(8,128)S(1)}, f32[6,48,256]{2,1,0:T(8,128)S(1)}, u32[]{:S(2)}, u32[]{:S(2)}) collective-permute-start(f32[6,48,256]{2,1,0:T(8,128)S(1)} %collective-permute-done.9.refs_2_), channel_id=1, source_target_pairs={{0,14},{1,3},{2,0},{3,5},{4,2},{5,7},{6,4},{7,9},{8,6},{9,11},{10,... | collective-permute-start | bytes 884744 | tf_op jit(solution)/shard_map/ppermute | solution.py:22
  60.2 6.7 %collective-permute-start.15 = (f32[6,48,256]{2,1,0:T(8,128)S(1)}, f32[6,48,256]{2,1,0:T(8,128)S(1)}, u32[]{:S(2)}, u32[]{:S(2)}) collective-permute-start(f32[6,48,256]{2,1,0:T(8,128)S(1)} %collective-permute-done.7.refs_1_), channel_id=1, source_target_pairs={{0,1},{1,0},{2,3},{3,2},{4,5},{5,4},{6,7},{7,6},{8,9},{9,8},{10,11... | collective-permute-start | bytes 884744 | tf_op jit(solution)/shard_map/ppermute | solution.py:22
  67.8 7.9 %collective-permute-start.25 = (f32[6,48,256]{2,1,0:T(8,128)S(1)}, f32[6,48,256]{2,1,0:T(8,128)S(1)}, u32[]{:S(2)}, u32[]{:S(2)}) collective-permute-start(f32[6,48,256]{2,1,0:T(8,128)S(1)} %collective-permute-done.12.refs_5_), channel_id=1, source_target_pairs={{0,2},{1,15},{2,4},{3,1},{4,6},{5,3},{6,8},{7,5},{8,10},{9,7},{10,... | collective-permute-start | bytes 884744 | tf_op jit(solution)/shard_map/ppermute | solution.py:22
  77.9 11.1 %collective-permute-start.17 = (f32[2,48,768]{2,1,0:T(8,128)S(1)}, f32[2,48,768]{2,1,0:T(8,128)}, u32[]{:S(2)}, u32[]{:S(2)}) collective-permute-start(f32[2,48,768]{2,1,0:T(8,128)S(1)} %get-tuple-element.47), channel_id=1, source_target_pairs={{0,2},{1,15},{2,4},{3,1},{4,6},{5,3},{6,8},{7,5},{8,10},{9,7},{10,... | collective-permute-start | bytes 884744 | tf_op jit(solution)/shard_map/ppermute | solution.py:22
  78.3 23.2 %collective-permute-start.21 = (f32[2,48,768]{2,1,0:T(8,128)S(1)}, f32[2,48,768]{2,1,0:T(8,128)S(1)}, u32[]{:S(2)}, u32[]{:S(2)}) collective-permute-start(f32[2,48,768]{2,1,0:T(8,128)S(1)} %dynamic-slice_bitcast_fusion), channel_id=1, source_target_pairs={{0,14},{1,3},{2,0},{3,5},{4,2},{5,7},{6,4},{7,9},{8,6},{9,11},{10,... | collective-permute-start | bytes 884744 | tf_op jit(solution)/shard_map/ppermute | solution.py:22
  82.4 7.7 %collective-permute-start.27 = (f32[3,2,2,32,128]{4,3,2,1,0:T(8,128)S(1)}, f32[3,2,2,32,128]{4,3,2,1,0:T(8,128)S(1)}, u32[]{:S(2)}, u32[]{:S(2)}) collective-permute-start(f32[3,2,2,32,128]{4,3,2,1,0:T(8,128)S(1)} %dynamic-slice_bitcast_fusion.1), channel_id=1, source_target_pairs={{0,64},{1,193},{2,66},{3,195},{4,68},{5,197},{6,70},{7,199},{8,72}... | collective-permute-start | bytes 589832 | tf_op jit(solution)/shard_map/ppermute | solution.py:22
  90.1 8.0 %collective-permute-start.18 = (f32[2,48,768]{2,1,0:T(8,128)S(1)}, f32[2,48,768]{2,1,0:T(8,128)S(1)}, u32[]{:S(2)}, u32[]{:S(2)}) collective-permute-start(f32[2,48,768]{2,1,0:T(8,128)S(1)} %bitcast_add_fusion.2), channel_id=1, source_target_pairs={{0,2},{1,15},{2,4},{3,1},{4,6},{5,3},{6,8},{7,5},{8,10},{9,7},{10,... | collective-permute-start | bytes 884744 | tf_op jit(solution)/shard_map/ppermute | solution.py:22
  90.3 8.0 %collective-permute-start.28 = (f32[3,2,32,128]{3,2,0,1:T(8,128)S(1)}, f32[3,2,32,128]{3,2,0,1:T(8,128)S(1)}, u32[]{:S(2)}, u32[]{:S(2)}) collective-permute-start(f32[3,2,32,128]{3,2,0,1:T(8,128)S(1)} %bitcast.74), channel_id=1, source_target_pairs={{0,128},{1,129},{2,130},{3,131},{4,132},{5,133},{6,134},{7,135},{8... | collective-permute-start | bytes 294920 | tf_op jit(solution)/shard_map/ppermute | solution.py:22
  98.1 11.2 %collective-permute-start.19 = (f32[2,48,768]{2,1,0:T(8,128)S(1)}, f32[2,48,768]{2,1,0:T(8,128)S(1)}, u32[]{:S(2)}, u32[]{:S(2)}) collective-permute-start(f32[2,48,768]{2,1,0:T(8,128)S(1)} %bitcast_add_fusion.3), channel_id=1, source_target_pairs={{0,2},{1,15},{2,4},{3,1},{4,6},{5,3},{6,8},{7,5},{8,10},{9,7},{10,... | collective-permute-start | bytes 884744 | tf_op jit(solution)/shard_map/ppermute | solution.py:22
  98.3 11.2 %collective-permute-start.29 = (f32[3,32,128]{2,1,0:T(8,128)S(1)}, f32[3,32,128]{2,1,0:T(8,128)S(1)}, u32[]{:S(2)}, u32[]{:S(2)}) collective-permute-start(f32[3,32,128]{2,1,0:T(8,128)S(1)} %dynamic-slice_bitcast_fusion.3), channel_id=1, source_target_pairs={{0,32},{1,33},{2,34},{3,35},{4,36},{5,37},{6,38},{7,39},{8,40},{9,... | collective-permute-start | bytes 147464 | tf_op jit(solution)/shard_map/ppermute | solution.py:22
  109.4 20.3 %collective-permute-start.22 = (f32[2,48,768]{2,1,0:T(8,128)S(1)}, f32[2,48,768]{2,1,0:T(8,128)S(1)}, u32[]{:S(2)}, u32[]{:S(2)}) collective-permute-start(f32[2,48,768]{2,1,0:T(8,128)S(1)} %get-tuple-element.55), channel_id=1, source_target_pairs={{0,14},{1,3},{2,0},{3,5},{4,2},{5,7},{6,4},{7,9},{8,6},{9,11},{10,... | collective-permute-start | bytes 884744 | tf_op jit(solution)/shard_map/ppermute | solution.py:22
  109.5 4.4 %collective-permute-start.30 = (f32[3,32,128]{2,1,0:T(8,128)S(1)}, f32[3,32,128]{2,1,0:T(8,128)S(1)}, u32[]{:S(2)}, u32[]{:S(2)}) collective-permute-start(f32[3,32,128]{2,1,0:T(8,128)S(1)} %bitcast_add_fusion.9), channel_id=1, source_target_pairs={{0,16},{1,17},{2,18},{3,19},{4,20},{5,21},{6,22},{7,23},{8,24},{9,... | collective-permute-start | bytes 147464 | tf_op jit(solution)/shard_map/ppermute | solution.py:22
  113.9 4.2 %collective-permute-start.31 = (f32[3,32,128]{2,1,0:T(8,128)S(1)}, f32[3,32,128]{2,1,0:T(8,128)S(1)}, u32[]{:S(2)}, u32[]{:S(2)}) collective-permute-start(f32[3,32,128]{2,1,0:T(8,128)S(1)} %add.237), channel_id=1, source_target_pairs={{0,2},{1,15},{2,0},{3,5},{4,6},{5,3},{6,4},{7,9},{8,10},{9,7},{10,... | collective-permute-start | bytes 147464 | tf_op jit(solution)/shard_map/ppermute | solution.py:22
  118.1 5.6 %collective-permute-start.32 = (f32[3,32,128]{2,1,0:T(8,128)S(1)}, f32[3,32,128]{2,1,0:T(8,128)S(1)}, u32[]{:S(2)}, u32[]{:S(2)}) collective-permute-start(f32[3,32,128]{2,1,0:T(8,128)S(1)} %add.238), channel_id=1, source_target_pairs={{0,4},{1,5},{2,6},{3,15},{4,0},{5,1},{6,2},{7,11},{8,12},{9,13},{1... | collective-permute-start | bytes 147464 | tf_op jit(solution)/shard_map/ppermute | solution.py:22
  123.7 8.2 %collective-permute-start.33 = (f32[3,32,128]{2,1,0:T(8,128)S(1)}, f32[3,32,128]{2,1,0:T(8,128)S(1)}, u32[]{:S(2)}, u32[]{:S(2)}) collective-permute-start(f32[3,32,128]{2,1,0:T(8,128)S(1)} %add.239), channel_id=1, source_target_pairs={{0,8},{1,9},{2,10},{3,11},{4,12},{5,13},{6,14},{7,15},{8,0},{9,1},... | collective-permute-start | bytes 147464 | tf_op jit(solution)/shard_map/ppermute | solution.py:22
  127.6 7.9 %collective-permute-start.20 = (f32[2,48,768]{2,1,0:T(8,128)S(1)}, f32[2,48,768]{2,1,0:T(8,128)S(1)}, u32[]{:S(2)}, u32[]{:S(2)}) collective-permute-start(f32[2,48,768]{2,1,0:T(8,128)S(1)} %get-tuple-element.54), channel_id=1, source_target_pairs={{0,2},{1,15},{2,4},{3,1},{4,6},{5,3},{6,8},{7,5},{8,10},{9,7},{10,... | collective-permute-start | bytes 884744 | tf_op jit(solution)/shard_map/ppermute | solution.py:22
  129.7 6.8 %collective-permute-start.23 = (f32[2,48,768]{2,1,0:T(8,128)S(1)}, f32[2,48,768]{2,1,0:T(8,128)S(1)}, u32[]{:S(2)}, u32[]{:S(2)}) collective-permute-start(f32[2,48,768]{2,1,0:T(8,128)S(1)} %bitcast_add_fusion.1), channel_id=1, source_target_pairs={{0,14},{1,3},{2,0},{3,5},{4,2},{5,7},{6,4},{7,9},{8,6},{9,11},{10,... | collective-permute-start | bytes 884744 | tf_op jit(solution)/shard_map/ppermute | solution.py:22
  136.6 5.9 %collective-permute-start.24 = (f32[48,768]{1,0:T(8,128)S(1)}, f32[48,768]{1,0:T(8,128)S(1)}, u32[]{:S(2)}, u32[]{:S(2)}) collective-permute-start(f32[48,768]{1,0:T(8,128)S(1)} %dynamic-slice_bitcast_fusion.2), channel_id=1, source_target_pairs={{0,16},{1,17},{2,18},{3,19},{4,20},{5,21},{6,22},{7,23},{8,24},{9,... | collective-permute-start | bytes 442376 | tf_op jit(solution)/shard_map/ppermute | solution.py:22
  (8 other events, 60.5 us)
where the time goes:
time: 146 us; the launch traced here: 143 us
  waiting for transfers between devices  80.7 us (55%)
  starting transfers between devices  44.5 us (30%)
  other arithmetic  7.08 us (5%)
  Pallas kernels  6.23 us (4%)
  local copies, waits for them, and re-layouts  3.54 us (2%)
    ppermute x35, waiting for transfers between devices, send(): return lax.ppermute(array, AXES, pairs)  80.7 us
    ppermute x35, starting transfers between devices, send(): return lax.ppermute(array, AXES, pairs)  44.5 us
    pallas_call x1, Pallas kernels, multiply(): pl.pallas_call(multiply_kernel, out_shape=[jax.ShapeDtypeStruct((size, wi...  4.17 us
  transfers between devices with their start and end apart: 35, of which 21 were waited for; matrix products, arithmetic and copies ran while one was open for 4% of the time, Pallas kernels for 3%

commit v1 on v0

--- a/solution.py
+++ b/solution.py
@@ -48,10 +48,6 @@
 
 def z_by(move):
     return lambda y, xh, xl, z, c: (y, xh, xl, (z + move(c)) % 8, c)
-
-
-def y_pair(y, xh, xl, z, c):
-    return (y ^ (3 if c else 1), xh, xl, z, c)
 
 
 def z_pair(bit):
@@ -129,7 +125,7 @@
     for j, piece in enumerate(pieces):
         dy, c = j % 4, (core if j < 4 else 1 - core)
         for dxh in range(2):
-            slot = ((y + 4 + (1 - 2 * c) * dy) % 4 * 2 + (xh + dxh) % 2) * 2 + c
+            slot = ((y + dy) % 4 * 2 + (xh + dxh) % 2) * 2 + c
             start = share_ref[column * 16 + slot] * rows
             for part in range(0, rows, SEGMENT):
                 place = pl.multiple_of(start + part, SEGMENT)
@@ -182,7 +178,7 @@
     row, col = lax.axis_index("row"), lax.axis_index("col")
     _, _, _, z, core = place_of(row, col)
     for d, part in enumerate(parts):
-        chip = (z + 8 + (1 - 2 * core) * d) % 8
+        chip = (z + d) % 8
         for x in range(2):
             here = slice((d * 2 + x) * rows, (d * 2 + x + 1) * rows)
             value = product[pl.ds(pl.multiple_of((x * 8 + chip) * rows, SEGMENT), rows), :]
@@ -234,7 +230,7 @@
 
 def per_device(inverse_block, factor_panel, diag_inverse, block_lists, list_counts):
     row, col = lax.axis_index("row"), lax.axis_index("col")
-    y, xh, xl, z, core = place_of(row, col)
+    _, _, xl, z, core = place_of(row, col)
     nsn, rows, width = factor_panel.shape
     span = inverse_block.shape[1]
 
@@ -243,37 +239,38 @@
 
     share = send(factor_panel, to_column)
     beside = send(factor_panel, other_xl)
-    after, beside = both(core, beside)
     halves = inverse_block.reshape(16, 2, rows, span)
-    s_own = pick(halves, after, 1).reshape(16 * rows, span)
-    s_other = facing(pick(halves, 1 - after, 1).reshape(16 * rows, span))
+    s_own, s_give = pick(halves, core, 1), pick(halves, 1 - core, 1)
+    s_own, s_other = s_own.reshape(16 * rows, span), facing(s_give.reshape(16 * rows, span))
     share, beside, s_other = both(share, beside, s_other)
 
     near = send(share, other_xh)
     line = jnp.concatenate(
         [jnp.where(xl == 0, factor_panel, beside), jnp.where(xl == 0, beside, factor_panel)]
     )
-    line_from1, line_to1 = send(line, z_by(ahead)), send(line, z_by(back))
+    line_down, line_up = send(line, z_by(lambda c: 1)), send(line, z_by(lambda c: -1))
     s_chip = jnp.concatenate(
         [jnp.where(core == 0, s_own, s_other), jnp.where(core == 0, s_other, s_own)], axis=1
     )
     s_high, s_low = split(s_chip)
     listed = listed_blocks(block_lists, list_counts, jnp.arange(block_lists.shape[1], dtype=jnp.int32))
     listed = listed.astype(jnp.int32)
-    near, line_from1, line_to1, s_high, s_low, listed = both(near, line_from1, line_to1, s_high, s_low, listed)
+    near, line_down, line_up, s_high, s_low, listed = both(near, line_down, line_up, s_high, s_low, listed)
 
     pair = jnp.concatenate([share, near])
-    from1, to1 = send(pair, y_by(ahead)), send(pair, y_by(back))
-    line_from2, line_to2 = send(line_from1, z_by(ahead)), send(line_to1, z_by(back))
+    below, above = send(pair, y_by(lambda c: 1)), send(pair, y_by(lambda c: -1))
+    line_down2, line_up2 = send(line_down, z_by(lambda c: 1)), send(line_up, z_by(lambda c: -1))
     pair_facing = facing(pair)
-    from1, to1, line_from2, line_to2, pair_facing = both(from1, to1, line_from2, line_to2, pair_facing)
-
-    far = send(from1, y_by(ahead))
-    line_from3, line_to3 = send(line_from2, z_by(ahead)), send(line_to2, z_by(back))
-    from1_facing, to1_facing = facing(from1), facing(to1)
-    far, line_from3, line_to3, from1_facing, to1_facing = both(far, line_from3, line_to3, from1_facing, to1_facing)
-    line_far = send(line_from3, z_by(ahead))
-    pieces = [pair, to1, far, from1, pair_facing, to1_facing, facing(far), from1_facing]
+    below, above, line_down2, line_up2, pair_facing = both(below, above, line_down2, line_up2, pair_facing)
+
+    far = send(jnp.where(core == 0, below, above), y_by(lambda c: 1 - 2 * c))
+    line_down3, line_up3 = send(line_down2, z_by(lambda c: 1)), send(line_up2, z_by(lambda c: -1))
+    below_facing, above_facing = facing(below), facing(above)
+    far, line_down3, line_up3, below_facing, above_facing = both(
+        far, line_down3, line_up3, below_facing, above_facing
+    )
+    line_far = send(jnp.where(core == 0, line_down3, line_up3), z_by(lambda c: 1 - 2 * c))
+    pieces = [pair, above, far, below, pair_facing, above_facing, facing(far), below_facing]
     product, opposite = multiply(listed, s_high, s_low, pieces)
     stacked = product.reshape(2, 8, rows, nsn * width)
 
@@ -293,12 +290,11 @@
     solved = -solved * mask[:, :, None]
 
     keep, give = diagonal_terms(
-        listed, product, [line, line_to1, line_to2, line_to3, line_far, line_from3, line_from2, line_from1]
-    )
-    terms = (keep + facing(give)).reshape(nsn, 2, 2, 2, width // 8, width // 2)
-    terms = pick(terms, y % 2, 2) + send(pick(terms, 1 - y % 2, 2), y_pair)
-    terms = pick(terms, y // 2, 1) + send(pick(terms, 1 - y // 2, 1), y_by(lambda c: 2))
-    terms = pick(terms, xh, 1) + send(pick(terms, 1 - xh, 1), other_xh)
+        listed, product, [line, line_up, line_up2, line_up3, line_far, line_down3, line_down2, line_down]
+    )
+    terms = (keep + facing(give)).reshape(nsn, 8, width // 8, width // 2).transpose(1, 0, 2, 3)
+    terms = lax.all_to_all(terms, "row", 0, 0, tiled=True)
+    terms = jnp.sum(terms, axis=0)
     terms = terms + send(terms, other_xl)
     terms = terms + send(terms, z_pair(1))
     terms = terms + send(terms, z_pair(2))

time: 146 us -> 140 us (0.959)
  the two profiles are of different devices: /device:TPU:6 before, /device:TPU:1 now
where the time goes in v1:
time: 140 us
  starting transfers between devices  62.6 us (45%)
  waiting for transfers between devices  48.8 us (35%)
  other arithmetic  11.4 us (8%)
  Pallas kernels  8.09 us (6%)
  local copies, waits for them, and re-layouts  7.95 us (6%)
    ppermute x32, starting transfers between devices, send(): return lax.ppermute(array, AXES, pairs)  56.2 us
    ppermute x32, waiting for transfers between devices, send(): return lax.ppermute(array, AXES, pairs)  42 us
    all_to_all x1, waiting for transfers between devices, per_device(): terms = lax.all_to_all(terms, 'row', 0, 0, tiled=True)  6.79 us
    all_to_all x1, starting transfers between devices, per_device(): terms = lax.all_to_all(terms, 'row', 0, 0, tiled=True)  6.35 us
    pallas_call x1, Pallas kernels, multiply(): pl.pallas_call(multiply_kernel, out_shape=[jax.ShapeDtypeStruct((size, wi...  4.86 us
    unnamed x27, local copies, waits for them, and re-layouts  4.6 us
    pallas_call x1, Pallas kernels, diagonal_terms(): pl.pallas_call(terms_kernel, out_shape=[jax.ShapeDtypeStruct((nsn, width,...  3.23 us
  transfers between devices with their start and end apart: 33, of which 17 were waited for; matrix products, arithmetic and copies ran while one was open for 8% of the time, Pallas kernels for 2%

profile of v1, /device:TPU:1, one launch (start us, length us, event | category | flops | bytes accessed | tf_op | source)
XLA Modules:
  0.0 139.8 jit_solution(12638818371521011260)
XLA Ops:
  0.7 1.8 %constant_dynamic-slice_fusion = (f32[16,1,48,384]{3,2,1,0:T(8,128)S(1)}, f32[16,1,48,384]{3,2,1,0:T(8,128)S(1)}) fusion(f32[16,2,48,384]{3,2,1,0:T(8,128)} %bitcast.60, s32[]{:T(128)S(6)} %select_n.146, s32[]{:T(128)S(6)} %select_n.140), kind=kLoop, calls=%fused_computation.36 | loop fusion | bytes 4718600 | tf_op jit(solution)/shard_map/jit(dynamic_index_in_dim)/dynamic_slice | solution.py:102
  2.5 3.3 %collective-permute-start.2 = (f32[768,384]{1,0:T(8,128)S(1)}, f32[768,384]{1,0:T(8,128)S(1)}, u32[]{:S(2)}, u32[]{:S(2)}) collective-permute-start(f32[768,384]{1,0:T(8,128)S(1)} %bitcast.62), channel_id=1, source_target_pairs={{0,1},{1,0},{2,3},{3,2},{4,5},{5,4},{6,7},{7,6},{8,9},{9,8},{10,11... | collective-permute-start | bytes 3538952 | tf_op jit(solution)/shard_map/ppermute | solution.py:22
  5.8 2.0 %collective-permute-start = (f32[3,48,256]{2,1,0:T(8,128)}, f32[3,48,256]{2,1,0:T(8,128)}, u32[]{:S(2)}, u32[]{:S(2)}) collective-permute-start(f32[3,48,256]{2,1,0:T(8,128)} %param.7), channel_id=1, source_target_pairs={{0,161},{1,97},{2,128},{3,224},{4,96},{5,0},{6,193},{7,33},{8,1},{... | collective-permute-start | bytes 442376 | tf_op jit(solution)/shard_map/ppermute | solution.py:22
  7.8 2.6 %collective-permute-start.1 = (f32[3,48,256]{2,1,0:T(8,128)}, f32[3,48,256]{2,1,0:T(8,128)}, u32[]{:S(2)}, u32[]{:S(2)}) collective-permute-start(f32[3,48,256]{2,1,0:T(8,128)} %param.7), channel_id=1, source_target_pairs={{0,16},{1,17},{2,18},{3,19},{4,20},{5,21},{6,22},{7,23},{8,24},{9,... | collective-permute-start | bytes 442376 | tf_op jit(solution)/shard_map/ppermute | solution.py:22
  10.8 5.4 %collective-permute-done = f32[3,48,256]{2,1,0:T(8,128)} collective-permute-done((f32[3,48,256]{2,1,0:T(8,128)}, f32[3,48,256]{2,1,0:T(8,128)}, u32[]{:S(2)}, u32[]{:S(2)}) %collective-permute-start) | collective-permute-done | bytes 147488 | tf_op jit(solution)/shard_map/ppermute | solution.py:22
  16.2 6.0 %collective-permute-done.1 = f32[3,48,256]{2,1,0:T(8,128)} collective-permute-done((f32[3,48,256]{2,1,0:T(8,128)}, f32[3,48,256]{2,1,0:T(8,128)}, u32[]{:S(2)}, u32[]{:S(2)}) %collective-permute-start.1) | collective-permute-done | bytes 147488 | tf_op jit(solution)/shard_map/ppermute | solution.py:22
  23.6 4.8 %collective-permute-start.4 = (f32[6,48,256]{2,1,0:T(8,128)S(1)}, f32[6,48,256]{2,1,0:T(8,128)S(1)}, u32[]{:S(2)}, u32[]{:S(2)}) collective-permute-start(f32[6,48,256]{2,1,0:T(8,128)S(1)} %pad_maximum_fusion.1.refs_0_), channel_id=1, source_target_pairs={{0,2},{1,3},{2,4},{3,5},{4,6},{5,7},{6,8},{7,9},{8,10},{9,11},{10,... | collective-permute-start | bytes 884744 | tf_op jit(solution)/shard_map/ppermute | solution.py:22
  28.4 4.4 %collective-permute-start.3 = (f32[3,48,256]{2,1,0:T(8,128)}, f32[3,48,256]{2,1,0:T(8,128)S(1)}, u32[]{:S(2)}, u32[]{:S(2)}) collective-permute-start(f32[3,48,256]{2,1,0:T(8,128)} %collective-permute-done), channel_id=1, source_target_pairs={{0,32},{1,33},{2,34},{3,35},{4,36},{5,37},{6,38},{7,39},{8,40},{9,... | collective-permute-start | bytes 442376 | tf_op jit(solution)/shard_map/ppermute | solution.py:22
  35.5 1.6 %collective-permute-done.3 = f32[3,48,256]{2,1,0:T(8,128)S(1)} collective-permute-done((f32[3,48,256]{2,1,0:T(8,128)}, f32[3,48,256]{2,1,0:T(8,128)S(1)}, u32[]{:S(2)}, u32[]{:S(2)}) %collective-permute-start.3) | collective-permute-done | bytes 147488 | tf_op jit(solution)/shard_map/ppermute | solution.py:22
  37.2 2.7 %collective-permute-start.7 = (f32[6,48,256]{2,1,0:T(8,128)S(1)}, f32[6,48,256]{2,1,0:T(8,128)S(1)}, u32[]{:S(2)}, u32[]{:S(2)}) collective-permute-start(f32[6,48,256]{2,1,0:T(8,128)S(1)} %constant_dynamic-update-slice_fusion.refs_0_), channel_id=1, source_target_pairs={{0,192},{1,193},{2,194},{3,195},{4,196},{5,197},{6,198},{7,199},{8... | collective-permute-start | bytes 884744 | tf_op jit(solution)/shard_map/ppermute | solution.py:22
  39.9 2.7 %collective-permute-start.9 = (f32[6,48,256]{2,1,0:T(8,128)S(1)}, f32[6,48,256]{2,1,0:T(8,128)S(1)}, u32[]{:S(2)}, u32[]{:S(2)}) collective-permute-start(f32[6,48,256]{2,1,0:T(8,128)S(1)} %collective-permute-done.5.refs_1_), channel_id=1, source_target_pairs={{0,14},{1,15},{2,0},{3,1},{4,2},{5,3},{6,4},{7,5},{8,6},{9,7},{10,... | collective-permute-start | bytes 884744 | tf_op jit(solution)/shard_map/ppermute | solution.py:22
  42.6 3.0 %collective-permute-start.10 = (f32[6,48,256]{2,1,0:T(8,128)S(1)}, f32[6,48,256]{2,1,0:T(8,128)S(1)}, u32[]{:S(2)}, u32[]{:S(2)}) collective-permute-start(f32[6,48,256]{2,1,0:T(8,128)S(1)} %constant_dynamic-update-slice_fusion.refs_0_), channel_id=1, source_target_pairs={{0,1},{1,0},{2,3},{3,2},{4,5},{5,4},{6,7},{7,6},{8,9},{9,8},{10,11... | collective-permute-start | bytes 884744 | tf_op jit(solution)/shard_map/ppermute | solution.py:22
  45.6 1.6 %collective-permute-done.8.refs_6_ = f32[6,48,256]{2,1,0:T(8,128)S(1)} collective-permute-done((f32[6,48,256]{2,1,0:T(8,128)S(1)}, f32[6,48,256]{2,1,0:T(8,128)S(1)}, u32[]{:S(2)}, u32[]{:S(2)}) %collective-permute-start.8) | collective-permute-done | bytes 294944 | tf_op jit(solution)/shard_map/ppermute | solution.py:22
  48.6 3.4 %collective-permute-start.12 = (f32[6,48,256]{2,1,0:T(8,128)S(1)}, f32[6,48,256]{2,1,0:T(8,128)S(1)}, u32[]{:S(2)}, u32[]{:S(2)}) collective-permute-start(f32[6,48,256]{2,1,0:T(8,128)S(1)} %collective-permute-done.8.refs_6_), channel_id=1, source_target_pairs={{0,2},{1,3},{2,4},{3,5},{4,6},{5,7},{6,8},{7,9},{8,10},{9,11},{10,... | collective-permute-start | bytes 884744 | tf_op jit(solution)/shard_map/ppermute | solution.py:22
  52.0 3.3 %collective-permute-start.14 = (f32[6,48,256]{2,1,0:T(8,128)S(1)}, f32[6,48,256]{2,1,0:T(8,128)S(1)}, u32[]{:S(2)}, u32[]{:S(2)}) collective-permute-start(f32[6,48,256]{2,1,0:T(8,128)S(1)} %collective-permute-done.6.refs_3_), channel_id=1, source_target_pairs={{0,1},{1,0},{2,3},{3,2},{4,5},{5,4},{6,7},{7,6},{8,9},{9,8},{10,11... | collective-permute-start | bytes 884744 | tf_op jit(solution)/shard_map/ppermute | solution.py:22
  55.7 3.3 %collective-permute-done.13.refs_3_ = f32[6,48,256]{2,1,0:T(8,128)S(1)} collective-permute-done((f32[6,48,256]{2,1,0:T(8,128)S(1)}, f32[6,48,256]{2,1,0:T(8,128)S(1)}, u32[]{:S(2)}, u32[]{:S(2)}) %collective-permute-start.13) | collective-permute-done | bytes 294944 | tf_op jit(solution)/shard_map/ppermute | solution.py:22
  59.0 3.3 %collective-permute-start.16 = (f32[6,48,256]{2,1,0:T(8,128)S(1)}, f32[6,48,256]{2,1,0:T(8,128)S(1)}, u32[]{:S(2)}, u32[]{:S(2)}) collective-permute-start(f32[6,48,256]{2,1,0:T(8,128)S(1)} %collective-permute-done.11.refs_2_), channel_id=1, source_target_pairs={{0,1},{1,0},{2,3},{3,2},{4,5},{5,4},{6,7},{7,6},{8,9},{9,8},{10,11... | collective-permute-start | bytes 884744 | tf_op jit(solution)/shard_map/ppermute | solution.py:22
  63.5 4.9 %multiply.1 = (f32[768,768]{1,0:T(8,128)S(1)}, f32[2,48,768]{2,1,0:T(8,128)}) custom-call(s32[256]{0:T(256)S(1)} %copy-done.8, s32[3,48]{1,0:T(4,128)S(1)} %convert_element_type.18.listed_ref, bf16[768,768]{1,0:T(8,128)(2,1)S(1)} %get-tuple-element.29.left_high, bf16[768,768]{1,0:T(8,128)(2,1)S(1)} %get-tuple-element.30.left_low, ...), custom_call_target="tpu_custom_call" | custom-call | flops 2717908992 | bytes 7077888 | tf_op jit(solution)/shard_map/multiply/pallas_call | solution.py:160
  69.8 5.7 %collective-permute-done.17 = f32[2,48,768]{2,1,0:T(8,128)} collective-permute-done((f32[2,48,768]{2,1,0:T(8,128)}, f32[2,48,768]{2,1,0:T(8,128)}, u32[]{:S(2)}, u32[]{:S(2)}) %collective-permute-start.17) | collective-permute-done | bytes 294944 | tf_op jit(solution)/shard_map/ppermute | solution.py:22
  75.5 1.7 %bitcast_add_fusion.2 = f32[2,48,768]{2,1,0:T(8,128)} fusion(f32[2,48,768]{2,1,0:T(8,128)} %collective-permute-done.17, f32[2,8,48,768]{3,2,1,0:T(8,128)S(1)} %bitcast.54, s32[]{:T(128)S(6)} %select_n.160), kind=kLoop, calls=%fused_computation.10 | loop fusion | flops 73728 | bytes 884740 | tf_op jit(solution)/shard_map/add | solution.py:281
  82.3 3.2 %terms.1 = (f32[3,256,128]{2,1,0:T(8,128)S(1)}, f32[3,256,128]{2,1,0:T(8,128)}) custom-call(s32[3,48]{1,0:T(4,128)S(1)} %convert_element_type.18.listed_ref, f32[768,768]{1,0:T(8,128)S(1)} %get-tuple-element.42.product, f32[6,48,256]{2,1,0:T(8,128)S(1)} %pad_maximum_fusion.1.refs_0_, f32[6,48,256]{2,1,0:T(8,128)S(1)} %copy-done.3, ...), custom_call_target="tpu_custom_call" | custom-call | flops 905969664 | bytes 4718592 | tf_op jit(solution)/shard_map/terms/pallas_call | solution.py:213
  86.2 3.3 %collective-permute-start.26 = (f32[3,256,128]{2,1,0:T(8,128)}, f32[3,256,128]{2,1,0:T(8,128)S(1)}, u32[]{:S(2)}, u32[]{:S(2)}) collective-permute-start(f32[3,256,128]{2,1,0:T(8,128)} %get-tuple-element.47), channel_id=1, source_target_pairs={{0,1},{1,0},{2,3},{3,2},{4,5},{5,4},{6,7},{7,6},{8,9},{9,8},{10,11... | collective-permute-start | bytes 1179656 | tf_op jit(solution)/shard_map/ppermute | solution.py:22
  91.9 6.3 %all-to-all-start = ((f32[8,3,32,128]{3,2,1,0:T(8,128)}), f32[8,3,32,128]{3,2,1,0:T(8,128)S(1)}, u32[]{:S(2)}, u32[]{:S(2)}) async-start(f32[8,3,32,128]{3,2,1,0:T(8,128)} %bitcast.53), calls=%async_computation | async-start | bytes 786432 | tf_op jit(solution)/shard_map/all_to_all | solution.py:296
  98.3 1.8 %bitcast_add_fusion.4 = (f32[2,48,768]{2,1,0:T(8,128)S(1)}, f32[2,48,768]{2,1,0:T(8,128)}) fusion(f32[2,48,768]{2,1,0:T(8,128)} %collective-permute-done.19, f32[2,8,48,768]{3,2,1,0:T(8,128)S(1)} %bitcast.57, s32[]{:T(128)S(6)} %select_n.156, f32[2,48,768]{2,1,0:T(8,128)} %collective-permute-done.21, s32[]{:T(128)S(6)} %select_n.164), kind=kLoop, calls=%fused_computation.12 | loop fusion | flops 147456 | bytes 1769480 | tf_op jit(solution)/shard_map/add | solution.py:283
  101.1 6.8 %all-to-all-done = f32[8,3,32,128]{3,2,1,0:T(8,128)S(1)} async-done(((f32[8,3,32,128]{3,2,1,0:T(8,128)}), f32[8,3,32,128]{3,2,1,0:T(8,128)S(1)}, u32[]{:S(2)}, u32[]{:S(2)}) %all-to-all-start) | async-done | bytes 393248 | tf_op jit(solution)/shard_map/all_to_all | solution.py:296
  108.0 2.9 %collective-permute-done.27 = f32[3,32,128]{2,1,0:T(8,128)S(1)} collective-permute-done((f32[3,32,128]{2,1,0:T(8,128)S(1)}, f32[3,32,128]{2,1,0:T(8,128)S(1)}, u32[]{:S(2)}, u32[]{:S(2)}) %collective-permute-start.27) | collective-permute-done | bytes 49184 | tf_op jit(solution)/shard_map/ppermute | solution.py:22
  111.1 4.1 %collective-permute-done.28 = f32[3,32,128]{2,1,0:T(8,128)S(1)} collective-permute-done((f32[3,32,128]{2,1,0:T(8,128)S(1)}, f32[3,32,128]{2,1,0:T(8,128)S(1)}, u32[]{:S(2)}, u32[]{:S(2)}) %collective-permute-start.28) | collective-permute-done | bytes 49184 | tf_op jit(solution)/shard_map/ppermute | solution.py:22
  115.8 2.7 %collective-permute-start.20 = (f32[2,48,768]{2,1,0:T(8,128)S(1)}, f32[2,48,768]{2,1,0:T(8,128)}, u32[]{:S(2)}, u32[]{:S(2)}) collective-permute-start(f32[2,48,768]{2,1,0:T(8,128)S(1)} %get-tuple-element.50), channel_id=1, source_target_pairs={{0,2},{1,15},{2,4},{3,1},{4,6},{5,3},{6,8},{7,5},{8,10},{9,7},{10,... | collective-permute-start | bytes 884744 | tf_op jit(solution)/shard_map/ppermute | solution.py:22
  119.3 3.7 %collective-permute-start.30 = (f32[3,32,128]{2,1,0:T(8,128)S(1)}, f32[3,32,128]{2,1,0:T(8,128)S(1)}, u32[]{:S(2)}, u32[]{:S(2)}) collective-permute-start(f32[3,32,128]{2,1,0:T(8,128)S(1)} %add.186), channel_id=1, source_target_pairs={{0,8},{1,9},{2,10},{3,11},{4,12},{5,13},{6,14},{7,15},{8,0},{9,1},... | collective-permute-start | bytes 147464 | tf_op jit(solution)/shard_map/ppermute | solution.py:22
  123.4 3.4 %collective-permute-done.30 = f32[3,32,128]{2,1,0:T(8,128)S(1)} collective-permute-done((f32[3,32,128]{2,1,0:T(8,128)S(1)}, f32[3,32,128]{2,1,0:T(8,128)S(1)}, u32[]{:S(2)}, u32[]{:S(2)}) %collective-permute-start.30) | collective-permute-done | bytes 49184 | tf_op jit(solution)/shard_map/ppermute | solution.py:22
  126.8 5.8 %collective-permute-start.31 = (f32[3,32,128]{2,1,0:T(8,128)S(1)}, f32[3,32,128]{2,1,0:T(8,128)S(1)}, u32[]{:S(2)}, u32[]{:S(2)}) collective-permute-start(f32[3,32,128]{2,1,0:T(8,128)S(1)} %add.187), channel_id=1, source_target_pairs={{0,1},{1,0},{2,3},{3,2},{4,5},{5,4},{6,7},{7,6},{8,9},{9,8},{10,11... | collective-permute-start | bytes 147464 | tf_op jit(solution)/shard_map/ppermute | solution.py:22
  135.2 3.7 %collective-permute-done.24 = f32[48,768]{1,0:T(8,128)S(1)} collective-permute-done((f32[48,768]{1,0:T(8,128)S(1)}, f32[48,768]{1,0:T(8,128)S(1)}, u32[]{:S(2)}, u32[]{:S(2)}) %collective-permute-start.24) | collective-permute-done | bytes 147488 | tf_op jit(solution)/shard_map/ppermute | solution.py:22
  (95 shorter events, 23.6 us)
Async XLA Ops:
  2.5 19.8 %collective-permute-start.2 = (f32[768,384]{1,0:T(8,128)S(1)}, f32[768,384]{1,0:T(8,128)S(1)}, u32[]{:S(2)}, u32[]{:S(2)}) collective-permute-start(f32[768,384]{1,0:T(8,128)S(1)} %bitcast.62), channel_id=1, source_target_pairs={{0,1},{1,0},{2,3},{3,2},{4,5},{5,4},{6,7},{7,6},{8,9},{9,8},{10,11... | collective-permute-start | bytes 3538952 | tf_op jit(solution)/shard_map/ppermute | solution.py:22
  5.8 10.5 %collective-permute-start = (f32[3,48,256]{2,1,0:T(8,128)}, f32[3,48,256]{2,1,0:T(8,128)}, u32[]{:S(2)}, u32[]{:S(2)}) collective-permute-start(f32[3,48,256]{2,1,0:T(8,128)} %param.7), channel_id=1, source_target_pairs={{0,161},{1,97},{2,128},{3,224},{4,96},{5,0},{6,193},{7,33},{8,1},{... | collective-permute-start | bytes 442376 | tf_op jit(solution)/shard_map/ppermute | solution.py:22
  7.8 14.4 %collective-permute-start.1 = (f32[3,48,256]{2,1,0:T(8,128)}, f32[3,48,256]{2,1,0:T(8,128)}, u32[]{:S(2)}, u32[]{:S(2)}) collective-permute-start(f32[3,48,256]{2,1,0:T(8,128)} %param.7), channel_id=1, source_target_pairs={{0,16},{1,17},{2,18},{3,19},{4,20},{5,21},{6,22},{7,23},{8,24},{9,... | collective-permute-start | bytes 442376 | tf_op jit(solution)/shard_map/ppermute | solution.py:22
  23.6 13.5 %collective-permute-start.4 = (f32[6,48,256]{2,1,0:T(8,128)S(1)}, f32[6,48,256]{2,1,0:T(8,128)S(1)}, u32[]{:S(2)}, u32[]{:S(2)}) collective-permute-start(f32[6,48,256]{2,1,0:T(8,128)S(1)} %pad_maximum_fusion.1.refs_0_), channel_id=1, source_target_pairs={{0,2},{1,3},{2,4},{3,5},{4,6},{5,7},{6,8},{7,9},{8,10},{9,11},{10,... | collective-permute-start | bytes 884744 | tf_op jit(solution)/shard_map/ppermute | solution.py:22
  28.4 8.8 %collective-permute-start.5 = (f32[6,48,256]{2,1,0:T(8,128)S(1)}, f32[6,48,256]{2,1,0:T(8,128)S(1)}, u32[]{:S(2)}, u32[]{:S(2)}) collective-permute-start(f32[6,48,256]{2,1,0:T(8,128)S(1)} %pad_maximum_fusion.1.refs_0_), channel_id=1, source_target_pairs={{0,14},{1,15},{2,0},{3,1},{4,2},{5,3},{6,4},{7,5},{8,6},{9,7},{10,... | collective-permute-start | bytes 884744 | tf_op jit(solution)/shard_map/ppermute | solution.py:22
  28.4 8.7 %collective-permute-start.3 = (f32[3,48,256]{2,1,0:T(8,128)}, f32[3,48,256]{2,1,0:T(8,128)S(1)}, u32[]{:S(2)}, u32[]{:S(2)}) collective-permute-start(f32[3,48,256]{2,1,0:T(8,128)} %collective-permute-done), channel_id=1, source_target_pairs={{0,32},{1,33},{2,34},{3,35},{4,36},{5,37},{6,38},{7,39},{8,40},{9,... | collective-permute-start | bytes 442376 | tf_op jit(solution)/shard_map/ppermute | solution.py:22
  37.1 8.5 %collective-permute-start.6 = (f32[6,48,256]{2,1,0:T(8,128)S(1)}, f32[6,48,256]{2,1,0:T(8,128)S(1)}, u32[]{:S(2)}, u32[]{:S(2)}) collective-permute-start(f32[6,48,256]{2,1,0:T(8,128)S(1)} %constant_dynamic-update-slice_fusion.refs_0_), channel_id=1, source_target_pairs={{0,64},{1,65},{2,66},{3,67},{4,68},{5,69},{6,70},{7,71},{8,72},{9,... | collective-permute-start | bytes 884744 | tf_op jit(solution)/shard_map/ppermute | solution.py:22
  37.2 8.4 %collective-permute-start.7 = (f32[6,48,256]{2,1,0:T(8,128)S(1)}, f32[6,48,256]{2,1,0:T(8,128)S(1)}, u32[]{:S(2)}, u32[]{:S(2)}) collective-permute-start(f32[6,48,256]{2,1,0:T(8,128)S(1)} %constant_dynamic-update-slice_fusion.refs_0_), channel_id=1, source_target_pairs={{0,192},{1,193},{2,194},{3,195},{4,196},{5,197},{6,198},{7,199},{8... | collective-permute-start | bytes 884744 | tf_op jit(solution)/shard_map/ppermute | solution.py:22
  39.9 7.3 %collective-permute-start.8 = (f32[6,48,256]{2,1,0:T(8,128)S(1)}, f32[6,48,256]{2,1,0:T(8,128)S(1)}, u32[]{:S(2)}, u32[]{:S(2)}) collective-permute-start(f32[6,48,256]{2,1,0:T(8,128)S(1)} %collective-permute-done.4.refs_7_), channel_id=1, source_target_pairs={{0,2},{1,3},{2,4},{3,5},{4,6},{5,7},{6,8},{7,9},{8,10},{9,11},{10,... | collective-permute-start | bytes 884744 | tf_op jit(solution)/shard_map/ppermute | solution.py:22
  39.9 7.9 %collective-permute-start.9 = (f32[6,48,256]{2,1,0:T(8,128)S(1)}, f32[6,48,256]{2,1,0:T(8,128)S(1)}, u32[]{:S(2)}, u32[]{:S(2)}) collective-permute-start(f32[6,48,256]{2,1,0:T(8,128)S(1)} %collective-permute-done.5.refs_1_), channel_id=1, source_target_pairs={{0,14},{1,15},{2,0},{3,1},{4,2},{5,3},{6,4},{7,5},{8,6},{9,7},{10,... | collective-permute-start | bytes 884744 | tf_op jit(solution)/shard_map/ppermute | solution.py:22
  42.6 5.2 %collective-permute-start.10 = (f32[6,48,256]{2,1,0:T(8,128)S(1)}, f32[6,48,256]{2,1,0:T(8,128)S(1)}, u32[]{:S(2)}, u32[]{:S(2)}) collective-permute-start(f32[6,48,256]{2,1,0:T(8,128)S(1)} %constant_dynamic-update-slice_fusion.refs_0_), channel_id=1, source_target_pairs={{0,1},{1,0},{2,3},{3,2},{4,5},{5,4},{6,7},{7,6},{8,9},{9,8},{10,11... | collective-permute-start | bytes 884744 | tf_op jit(solution)/shard_map/ppermute | solution.py:22
  47.8 7.5 %collective-permute-start.11 = (f32[6,48,256]{2,1,0:T(8,128)S(1)}, f32[6,48,256]{2,1,0:T(8,128)S(1)}, u32[]{:S(2)}, u32[]{:S(2)}) collective-permute-start(f32[6,48,256]{2,1,0:T(8,128)S(1)} %broadcast_select_fusion.1), channel_id=1, source_target_pairs={{0,64},{1,193},{2,66},{3,195},{4,68},{5,197},{6,70},{7,199},{8,72}... | collective-permute-start | bytes 884744 | tf_op jit(solution)/shard_map/ppermute | solution.py:22
  48.6 7.1 %collective-permute-start.12 = (f32[6,48,256]{2,1,0:T(8,128)S(1)}, f32[6,48,256]{2,1,0:T(8,128)S(1)}, u32[]{:S(2)}, u32[]{:S(2)}) collective-permute-start(f32[6,48,256]{2,1,0:T(8,128)S(1)} %collective-permute-done.8.refs_6_), channel_id=1, source_target_pairs={{0,2},{1,3},{2,4},{3,5},{4,6},{5,7},{6,8},{7,9},{8,10},{9,11},{10,... | collective-permute-start | bytes 884744 | tf_op jit(solution)/shard_map/ppermute | solution.py:22
  52.0 7.0 %collective-permute-start.13 = (f32[6,48,256]{2,1,0:T(8,128)S(1)}, f32[6,48,256]{2,1,0:T(8,128)S(1)}, u32[]{:S(2)}, u32[]{:S(2)}) collective-permute-start(f32[6,48,256]{2,1,0:T(8,128)S(1)} %collective-permute-done.9.refs_2_), channel_id=1, source_target_pairs={{0,14},{1,15},{2,0},{3,1},{4,2},{5,3},{6,4},{7,5},{8,6},{9,7},{10,... | collective-permute-start | bytes 884744 | tf_op jit(solution)/shard_map/ppermute | solution.py:22
  52.0 7.0 %collective-permute-start.14 = (f32[6,48,256]{2,1,0:T(8,128)S(1)}, f32[6,48,256]{2,1,0:T(8,128)S(1)}, u32[]{:S(2)}, u32[]{:S(2)}) collective-permute-start(f32[6,48,256]{2,1,0:T(8,128)S(1)} %collective-permute-done.6.refs_3_), channel_id=1, source_target_pairs={{0,1},{1,0},{2,3},{3,2},{4,5},{5,4},{6,7},{7,6},{8,9},{9,8},{10,11... | collective-permute-start | bytes 884744 | tf_op jit(solution)/shard_map/ppermute | solution.py:22
  55.3 3.7 %collective-permute-start.15 = (f32[6,48,256]{2,1,0:T(8,128)S(1)}, f32[6,48,256]{2,1,0:T(8,128)S(1)}, u32[]{:S(2)}, u32[]{:S(2)}) collective-permute-start(f32[6,48,256]{2,1,0:T(8,128)S(1)} %collective-permute-done.7.refs_1_), channel_id=1, source_target_pairs={{0,1},{1,0},{2,3},{3,2},{4,5},{5,4},{6,7},{7,6},{8,9},{9,8},{10,11... | collective-permute-start | bytes 884744 | tf_op jit(solution)/shard_map/ppermute | solution.py:22
  59.0 4.5 %collective-permute-start.16 = (f32[6,48,256]{2,1,0:T(8,128)S(1)}, f32[6,48,256]{2,1,0:T(8,128)S(1)}, u32[]{:S(2)}, u32[]{:S(2)}) collective-permute-start(f32[6,48,256]{2,1,0:T(8,128)S(1)} %collective-permute-done.11.refs_2_), channel_id=1, source_target_pairs={{0,1},{1,0},{2,3},{3,2},{4,5},{5,4},{6,7},{7,6},{8,9},{9,8},{10,11... | collective-permute-start | bytes 884744 | tf_op jit(solution)/shard_map/ppermute | solution.py:22
  68.4 7.1 %collective-permute-start.17 = (f32[2,48,768]{2,1,0:T(8,128)}, f32[2,48,768]{2,1,0:T(8,128)}, u32[]{:S(2)}, u32[]{:S(2)}) collective-permute-start(f32[2,48,768]{2,1,0:T(8,128)} %get-tuple-element.43), channel_id=1, source_target_pairs={{0,2},{1,15},{2,4},{3,1},{4,6},{5,3},{6,8},{7,5},{8,10},{9,7},{10,... | collective-permute-start | bytes 884744 | tf_op jit(solution)/shard_map/ppermute | solution.py:22
  69.8 9.6 %collective-permute-start.25 = (f32[6,48,256]{2,1,0:T(8,128)}, f32[6,48,256]{2,1,0:T(8,128)}, u32[]{:S(2)}, u32[]{:S(2)}) collective-permute-start(f32[6,48,256]{2,1,0:T(8,128)} %broadcast_select_fusion), channel_id=1, source_target_pairs={{0,2},{1,15},{2,4},{3,1},{4,6},{5,3},{6,8},{7,5},{8,10},{9,7},{10,... | collective-permute-start | bytes 884744 | tf_op jit(solution)/shard_map/ppermute | solution.py:22
  77.2 12.4 %collective-permute-start.18 = (f32[2,48,768]{2,1,0:T(8,128)}, f32[2,48,768]{2,1,0:T(8,128)}, u32[]{:S(2)}, u32[]{:S(2)}) collective-permute-start(f32[2,48,768]{2,1,0:T(8,128)} %bitcast_add_fusion.2), channel_id=1, source_target_pairs={{0,2},{1,15},{2,4},{3,1},{4,6},{5,3},{6,8},{7,5},{8,10},{9,7},{10,... | collective-permute-start | bytes 884744 | tf_op jit(solution)/shard_map/ppermute | solution.py:22
  78.6 19.7 %collective-permute-start.21 = (f32[2,48,768]{2,1,0:T(8,128)}, f32[2,48,768]{2,1,0:T(8,128)}, u32[]{:S(2)}, u32[]{:S(2)}) collective-permute-start(f32[2,48,768]{2,1,0:T(8,128)} %dynamic-slice_bitcast_fusion), channel_id=1, source_target_pairs={{0,14},{1,3},{2,0},{3,5},{4,2},{5,7},{6,4},{7,9},{8,6},{9,11},{10,... | collective-permute-start | bytes 884744 | tf_op jit(solution)/shard_map/ppermute | solution.py:22
  86.2 4.8 %collective-permute-start.26 = (f32[3,256,128]{2,1,0:T(8,128)}, f32[3,256,128]{2,1,0:T(8,128)S(1)}, u32[]{:S(2)}, u32[]{:S(2)}) collective-permute-start(f32[3,256,128]{2,1,0:T(8,128)} %get-tuple-element.47), channel_id=1, source_target_pairs={{0,1},{1,0},{2,3},{3,2},{4,5},{5,4},{6,7},{7,6},{8,9},{9,8},{10,11... | collective-permute-start | bytes 1179656 | tf_op jit(solution)/shard_map/ppermute | solution.py:22
  90.5 7.8 %collective-permute-start.19 = (f32[2,48,768]{2,1,0:T(8,128)S(1)}, f32[2,48,768]{2,1,0:T(8,128)}, u32[]{:S(2)}, u32[]{:S(2)}) collective-permute-start(f32[2,48,768]{2,1,0:T(8,128)S(1)} %bitcast_add_fusion.3), channel_id=1, source_target_pairs={{0,2},{1,15},{2,4},{3,1},{4,6},{5,3},{6,8},{7,5},{8,10},{9,7},{10,... | collective-permute-start | bytes 884744 | tf_op jit(solution)/shard_map/ppermute | solution.py:22
  91.9 16.0 %all-to-all-start = ((f32[8,3,32,128]{3,2,1,0:T(8,128)}), f32[8,3,32,128]{3,2,1,0:T(8,128)S(1)}, u32[]{:S(2)}, u32[]{:S(2)}) async-start(f32[8,3,32,128]{3,2,1,0:T(8,128)} %bitcast.53), calls=%async_computation | async-start | bytes 786432 | tf_op jit(solution)/shard_map/all_to_all | solution.py:296
  100.1 22.8 %collective-permute-start.22 = (f32[2,48,768]{2,1,0:T(8,128)}, f32[2,48,768]{2,1,0:T(8,128)S(1)}, u32[]{:S(2)}, u32[]{:S(2)}) collective-permute-start(f32[2,48,768]{2,1,0:T(8,128)} %get-tuple-element.51), channel_id=1, source_target_pairs={{0,14},{1,3},{2,0},{3,5},{4,2},{5,7},{6,4},{7,9},{8,6},{9,11},{10,... | collective-permute-start | bytes 884744 | tf_op jit(solution)/shard_map/ppermute | solution.py:22
  111.0 4.2 %collective-permute-start.28 = (f32[3,32,128]{2,1,0:T(8,128)S(1)}, f32[3,32,128]{2,1,0:T(8,128)S(1)}, u32[]{:S(2)}, u32[]{:S(2)}) collective-permute-start(f32[3,32,128]{2,1,0:T(8,128)S(1)} %add.184), channel_id=1, source_target_pairs={{0,2},{1,15},{2,0},{3,5},{4,6},{5,3},{6,4},{7,9},{8,10},{9,7},{10,... | collective-permute-start | bytes 147464 | tf_op jit(solution)/shard_map/ppermute | solution.py:22
  115.2 4.0 %collective-permute-start.29 = (f32[3,32,128]{2,1,0:T(8,128)S(1)}, f32[3,32,128]{2,1,0:T(8,128)S(1)}, u32[]{:S(2)}, u32[]{:S(2)}) collective-permute-start(f32[3,32,128]{2,1,0:T(8,128)S(1)} %add.185), channel_id=1, source_target_pairs={{0,4},{1,5},{2,6},{3,15},{4,0},{5,1},{6,2},{7,11},{8,12},{9,13},{1... | collective-permute-start | bytes 147464 | tf_op jit(solution)/shard_map/ppermute | solution.py:22
  115.8 17.6 %collective-permute-start.20 = (f32[2,48,768]{2,1,0:T(8,128)S(1)}, f32[2,48,768]{2,1,0:T(8,128)}, u32[]{:S(2)}, u32[]{:S(2)}) collective-permute-start(f32[2,48,768]{2,1,0:T(8,128)S(1)} %get-tuple-element.50), channel_id=1, source_target_pairs={{0,2},{1,15},{2,4},{3,1},{4,6},{5,3},{6,8},{7,5},{8,10},{9,7},{10,... | collective-permute-start | bytes 884744 | tf_op jit(solution)/shard_map/ppermute | solution.py:22
  119.3 7.5 %collective-permute-start.30 = (f32[3,32,128]{2,1,0:T(8,128)S(1)}, f32[3,32,128]{2,1,0:T(8,128)S(1)}, u32[]{:S(2)}, u32[]{:S(2)}) collective-permute-start(f32[3,32,128]{2,1,0:T(8,128)S(1)} %add.186), channel_id=1, source_target_pairs={{0,8},{1,9},{2,10},{3,11},{4,12},{5,13},{6,14},{7,15},{8,0},{9,1},... | collective-permute-start | bytes 147464 | tf_op jit(solution)/shard_map/ppermute | solution.py:22
  123.0 10.4 %collective-permute-start.23 = (f32[2,48,768]{2,1,0:T(8,128)S(1)}, f32[2,48,768]{2,1,0:T(8,128)S(1)}, u32[]{:S(2)}, u32[]{:S(2)}) collective-permute-start(f32[2,48,768]{2,1,0:T(8,128)S(1)} %bitcast_add_fusion.1), channel_id=1, source_target_pairs={{0,14},{1,3},{2,0},{3,5},{4,2},{5,7},{6,4},{7,9},{8,6},{9,11},{10,... | collective-permute-start | bytes 884744 | tf_op jit(solution)/shard_map/ppermute | solution.py:22
  126.8 6.6 %collective-permute-start.31 = (f32[3,32,128]{2,1,0:T(8,128)S(1)}, f32[3,32,128]{2,1,0:T(8,128)S(1)}, u32[]{:S(2)}, u32[]{:S(2)}) collective-permute-start(f32[3,32,128]{2,1,0:T(8,128)S(1)} %add.187), channel_id=1, source_target_pairs={{0,1},{1,0},{2,3},{3,2},{4,5},{5,4},{6,7},{7,6},{8,9},{9,8},{10,11... | collective-permute-start | bytes 147464 | tf_op jit(solution)/shard_map/ppermute | solution.py:22
  134.5 4.5 %collective-permute-start.24 = (f32[48,768]{1,0:T(8,128)S(1)}, f32[48,768]{1,0:T(8,128)S(1)}, u32[]{:S(2)}, u32[]{:S(2)}) collective-permute-start(f32[48,768]{1,0:T(8,128)S(1)} %dynamic-slice_bitcast_fusion.1), channel_id=1, source_target_pairs={{0,16},{1,17},{2,18},{3,19},{4,20},{5,21},{6,22},{7,23},{8,24},{9,... | collective-permute-start | bytes 442376 | tf_op jit(solution)/shard_map/ppermute | solution.py:22
  (14 other events, 130.7 us)

commit v2 on v1

--- a/solution.py
+++ b/solution.py
@@ -117,7 +117,7 @@
 
 
 def multiply_kernel(share_ref, listed_ref, left_high, left_low, *refs):
-    pieces, (out, opposite, right_high, right_low) = refs[:8], refs[8:]
+    pieces, chunks, (out, right_high, right_low) = refs[:8], refs[8:16], refs[16:]
     nsn, rows, width = pieces[0].shape[0] // 2, pieces[0].shape[1], pieces[0].shape[2]
     depth = right_high.shape[0]
     y, xh, xl, z, core = place_of(lax.axis_index("row"), lax.axis_index("col"))
@@ -147,8 +147,10 @@
             + dot(left_high[band, :], right_low[...])
             + dot(left_low[band, :], right_high[...])
         )
-    for x in range(2):
-        opposite[x] = out[pl.ds(pl.multiple_of((x * 8 + (z + 4) % 8) * rows, SEGMENT), rows), :]
+    for j, chunk in enumerate(chunks):
+        chip = (z + 8 + (1 - 2 * core) * j) % 8
+        for x in range(2):
+            chunk[x] = out[pl.ds(pl.multiple_of((x * 8 + chip) * rows, SEGMENT), rows), :]
 
 
 def multiply(listed, left_high, left_low, pieces):
@@ -159,21 +161,18 @@
     scalars = pl.BlockSpec(memory_space=pltpu.SMEM)
     return pl.pallas_call(
         multiply_kernel,
-        out_shape=[
-            jax.ShapeDtypeStruct((size, wide), jnp.float32),
-            jax.ShapeDtypeStruct((2, rows, wide), jnp.float32),
-        ],
+        out_shape=[jax.ShapeDtypeStruct((2, rows, wide), jnp.float32)] * 8,
         in_specs=[scalars, scalars] + [whole] * (2 + len(pieces)),
-        out_specs=[whole, whole],
-        scratch_shapes=[pltpu.VMEM((depth, wide), jnp.bfloat16)] * 2,
+        out_specs=[whole] * 8,
+        scratch_shapes=[pltpu.VMEM((size, wide), jnp.float32)] + [pltpu.VMEM((depth, wide), jnp.bfloat16)] * 2,
         compiler_params=pltpu.CompilerParams(vmem_limit_bytes=VMEM_LIMIT),
         cost_estimate=pl.CostEstimate(flops=6 * size * wide * depth, bytes_accessed=12 * size * wide, transcendentals=0),
         name="multiply",
     )(jnp.asarray(np.array(SHARES, np.int32).reshape(-1)), listed, left_high, left_low, *pieces)
 
 
-def terms_kernel(listed_ref, product, *refs):
-    parts, (keep, give, left_high, left_low, right_high, right_low) = refs[:8], refs[8:]
+def terms_kernel(listed_ref, *refs):
+    chunks, parts, (keep, give, left_high, left_low, right_high, right_low) = refs[:8], refs[8:16], refs[16:]
     nsn, rows, width = parts[0].shape[0] // 2, parts[0].shape[1], parts[0].shape[2]
     row, col = lax.axis_index("row"), lax.axis_index("col")
     _, _, _, z, core = place_of(row, col)
@@ -181,7 +180,7 @@
         chip = (z + d) % 8
         for x in range(2):
             here = slice((d * 2 + x) * rows, (d * 2 + x + 1) * rows)
-            value = product[pl.ds(pl.multiple_of((x * 8 + chip) * rows, SEGMENT), rows), :]
+            value = jnp.where(core == 0, chunks[d][x], chunks[-d % 8][x])
             right_high[here, :], right_low[here, :] = split_value(value)
             first = (row * 32 + x * 16 + chip * 2 + core) * rows
             for s in range(0, rows, SEGMENT):
@@ -202,18 +201,19 @@
             dot(left_high, right_high, lanes) + dot(left_high, right_low, lanes) + dot(left_low, right_high, lanes)
         )
         below, above = value[:, : width // 2], value[:, width // 2 :]
-        keep[k] = jnp.where(core == 0, below, above)
-        give[k] = jnp.where(core == 0, above, below)
-
-
-def diagonal_terms(listed, product, parts):
-    size, wide = product.shape
+        shape = keep.shape[:1] + keep.shape[2:]
+        keep[:, k] = jnp.where(core == 0, below, above).reshape(shape)
+        give[:, k] = jnp.where(core == 0, above, below).reshape(shape)
+
+
+def diagonal_terms(listed, chunks, parts):
     nsn, width = parts[0].shape[0] // 2, parts[0].shape[2]
+    size, wide = 8 * 2 * parts[0].shape[1], nsn * width
     whole = pl.BlockSpec(memory_space=pltpu.VMEM)
     return pl.pallas_call(
         terms_kernel,
-        out_shape=[jax.ShapeDtypeStruct((nsn, width, width // 2), jnp.float32)] * 2,
-        in_specs=[pl.BlockSpec(memory_space=pltpu.SMEM)] + [whole] * (1 + len(parts)),
+        out_shape=[jax.ShapeDtypeStruct((8, nsn, width // 8, width // 2), jnp.float32)] * 2,
+        in_specs=[pl.BlockSpec(memory_space=pltpu.SMEM)] + [whole] * (len(chunks) + len(parts)),
         out_specs=[whole, whole],
         scratch_shapes=[pltpu.VMEM((size, wide), jnp.bfloat16)] * 4,
         compiler_params=pltpu.CompilerParams(vmem_limit_bytes=VMEM_LIMIT),
@@ -221,7 +221,7 @@
             flops=6 * size * wide * width, bytes_accessed=8 * size * wide, transcendentals=0
         ),
         name="terms",
-    )(listed, product, *parts)
+    )(listed, *chunks, *parts)
 
 
 def both(*arrays):
@@ -230,7 +230,7 @@
 
 def per_device(inverse_block, factor_panel, diag_inverse, block_lists, list_counts):
     row, col = lax.axis_index("row"), lax.axis_index("col")
-    _, _, xl, z, core = place_of(row, col)
+    _, _, xl, _, core = place_of(row, col)
     nsn, rows, width = factor_panel.shape
     span = inverse_block.shape[1]
 
@@ -271,17 +271,13 @@
     )
     line_far = send(jnp.where(core == 0, line_down3, line_up3), z_by(lambda c: 1 - 2 * c))
     pieces = [pair, above, far, below, pair_facing, above_facing, facing(far), below_facing]
-    product, opposite = multiply(listed, s_high, s_low, pieces)
-    stacked = product.reshape(2, 8, rows, nsn * width)
-
-    def at(distance):
-        return pick(stacked, (z + (1 - 2 * core) * distance) % 8, 1)
-
-    opposite = send(opposite, z_by(ahead))
-    first, second = send(at(3) + opposite, z_by(ahead)), send(at(-3), z_by(back))
-    first, second = send(at(2) + first, z_by(ahead)), send(at(-2) + second, z_by(back))
-    first, second = send(at(1) + first, z_by(ahead)), send(at(-1) + second, z_by(back))
-    partial = at(0) + first + second
+    chunks = multiply(listed, s_high, s_low, pieces)
+
+    first = send(chunks[4], z_by(ahead))
+    first, second = send(chunks[3] + first, z_by(ahead)), send(chunks[5], z_by(back))
+    first, second = send(chunks[2] + first, z_by(ahead)), send(chunks[6] + second, z_by(back))
+    first, second = send(chunks[1] + first, z_by(ahead)), send(chunks[7] + second, z_by(back))
+    partial = chunks[0] + first + second
     crossed = send(pick(partial, 1 - xl, 0), other_xl)
     total = pick(partial, xl, 0) + crossed
     row_blocks = ((row * 32 + col) * rows + jnp.arange(rows, dtype=jnp.int32)) // BLK
@@ -290,9 +286,9 @@
     solved = -solved * mask[:, :, None]
 
     keep, give = diagonal_terms(
-        listed, product, [line, line_up, line_up2, line_up3, line_far, line_down3, line_down2, line_down]
-    )
-    terms = (keep + facing(give)).reshape(nsn, 8, width // 8, width // 2).transpose(1, 0, 2, 3)
+        listed, chunks, [line, line_up, line_up2, line_up3, line_far, line_down3, line_down2, line_down]
+    )
+    terms = keep + facing(give)
     terms = lax.all_to_all(terms, "row", 0, 0, tiled=True)
     terms = jnp.sum(terms, axis=0)
     terms = terms + send(terms, other_xl)

time: 140 us -> 132 us (0.943)
  the two profiles are of different devices: /device:TPU:1 before, /device:TPU:6 now
where the time goes in v2:
time: 132 us; the launch traced here: 130 us
  waiting for transfers between devices  61.8 us (47%)
  starting transfers between devices  53.1 us (40%)
  Pallas kernels  6.43 us (5%)
  other arithmetic  4.49 us (3%)
  local copies, waits for them, and re-layouts  2.78 us (2%)
    ppermute x32, waiting for transfers between devices, send(): return lax.ppermute(array, AXES, pairs)  58.5 us
    ppermute x32, starting transfers between devices, send(): return lax.ppermute(array, AXES, pairs)  44.8 us
    all_to_all x1, starting transfers between devices, per_device(): terms = lax.all_to_all(terms, 'row', 0, 0, tiled=True)  8.23 us
    pallas_call x1, Pallas kernels, multiply(): pl.pallas_call(multiply_kernel, out_shape=[jax.ShapeDtypeStruct((2, rows,...  4.27 us
    all_to_all x1, waiting for transfers between devices, per_device(): terms = lax.all_to_all(terms, 'row', 0, 0, tiled=True)  3.36 us
  transfers between devices with their start and end apart: 33, of which 18 were waited for; matrix products, arithmetic and copies ran while one was open for 3% of the time, Pallas kernels for 3%

profile of v2, /device:TPU:6, one launch (start us, length us, event | category | flops | bytes accessed | tf_op | source)
XLA Modules:
  0.0 129.6 jit_solution(14207232189763146878)
XLA Ops:
  0.7 1.8 %constant_dynamic-slice_fusion = (f32[16,1,48,384]{3,2,1,0:T(8,128)S(1)}, f32[16,1,48,384]{3,2,1,0:T(8,128)S(1)}) fusion(f32[16,2,48,384]{3,2,1,0:T(8,128)} %bitcast.19, s32[]{:T(128)S(6)} %select_n.89, s32[]{:T(128)S(6)} %select_n.83), kind=kLoop, calls=%fused_computation.33 | loop fusion | bytes 4718600 | tf_op jit(solution)/shard_map/jit(dynamic_index_in_dim)/dynamic_slice | solution.py:102
  2.6 5.7 %collective-permute-start = (f32[3,48,256]{2,1,0:T(8,128)}, f32[3,48,256]{2,1,0:T(8,128)}, u32[]{:S(2)}, u32[]{:S(2)}) collective-permute-start(f32[3,48,256]{2,1,0:T(8,128)} %param.7), channel_id=1, source_target_pairs={{0,161},{1,97},{2,128},{3,224},{4,96},{5,0},{6,193},{7,33},{8,1},{... | collective-permute-start | bytes 442376 | tf_op jit(solution)/shard_map/ppermute | solution.py:22
  8.6 16.8 %collective-permute-done = f32[3,48,256]{2,1,0:T(8,128)} collective-permute-done((f32[3,48,256]{2,1,0:T(8,128)}, f32[3,48,256]{2,1,0:T(8,128)}, u32[]{:S(2)}, u32[]{:S(2)}) %collective-permute-start) | collective-permute-done | bytes 147488 | tf_op jit(solution)/shard_map/ppermute | solution.py:22
  26.6 3.2 %collective-permute-start.5 = (f32[6,48,256]{2,1,0:T(8,128)S(1)}, f32[6,48,256]{2,1,0:T(8,128)S(1)}, u32[]{:S(2)}, u32[]{:S(2)}) collective-permute-start(f32[6,48,256]{2,1,0:T(8,128)S(1)} %pad_maximum_fusion.1.refs_8_), channel_id=1, source_target_pairs={{0,14},{1,15},{2,0},{3,1},{4,2},{5,3},{6,4},{7,5},{8,6},{9,7},{10,... | collective-permute-start | bytes 884744 | tf_op jit(solution)/shard_map/ppermute | solution.py:22
  32.6 4.1 %collective-permute-done.3 = f32[3,48,256]{2,1,0:T(8,128)S(1)} collective-permute-done((f32[3,48,256]{2,1,0:T(8,128)}, f32[3,48,256]{2,1,0:T(8,128)S(1)}, u32[]{:S(2)}, u32[]{:S(2)}) %collective-permute-start.3) | collective-permute-done | bytes 147488 | tf_op jit(solution)/shard_map/ppermute | solution.py:22
  36.8 3.2 %collective-permute-start.7 = (f32[6,48,256]{2,1,0:T(8,128)S(1)}, f32[6,48,256]{2,1,0:T(8,128)S(1)}, u32[]{:S(2)}, u32[]{:S(2)}) collective-permute-start(f32[6,48,256]{2,1,0:T(8,128)S(1)} %constant_dynamic-update-slice_fusion.refs_0_), channel_id=1, source_target_pairs={{0,192},{1,193},{2,194},{3,195},{4,196},{5,197},{6,198},{7,199},{8... | collective-permute-start | bytes 884744 | tf_op jit(solution)/shard_map/ppermute | solution.py:22
  40.0 3.2 %collective-permute-start.9 = (f32[6,48,256]{2,1,0:T(8,128)S(1)}, f32[6,48,256]{2,1,0:T(8,128)S(1)}, u32[]{:S(2)}, u32[]{:S(2)}) collective-permute-start(f32[6,48,256]{2,1,0:T(8,128)S(1)} %collective-permute-done.5.refs_9_), channel_id=1, source_target_pairs={{0,14},{1,15},{2,0},{3,1},{4,2},{5,3},{6,4},{7,5},{8,6},{9,7},{10,... | collective-permute-start | bytes 884744 | tf_op jit(solution)/shard_map/ppermute | solution.py:22
  44.7 3.2 %collective-permute-done.8.refs_14_ = f32[6,48,256]{2,1,0:T(8,128)S(1)} collective-permute-done((f32[6,48,256]{2,1,0:T(8,128)S(1)}, f32[6,48,256]{2,1,0:T(8,128)S(1)}, u32[]{:S(2)}, u32[]{:S(2)}) %collective-permute-start.8) | collective-permute-done | bytes 294944 | tf_op jit(solution)/shard_map/ppermute | solution.py:22
  48.1 1.8 %collective-permute-start.12 = (f32[6,48,256]{2,1,0:T(8,128)S(1)}, f32[6,48,256]{2,1,0:T(8,128)S(1)}, u32[]{:S(2)}, u32[]{:S(2)}) collective-permute-start(f32[6,48,256]{2,1,0:T(8,128)S(1)} %collective-permute-done.8.refs_14_), channel_id=1, source_target_pairs={{0,2},{1,3},{2,4},{3,5},{4,6},{5,7},{6,8},{7,9},{8,10},{9,11},{10,... | collective-permute-start | bytes 884744 | tf_op jit(solution)/shard_map/ppermute | solution.py:22
  49.9 1.6 %collective-permute-start.13 = (f32[6,48,256]{2,1,0:T(8,128)S(1)}, f32[6,48,256]{2,1,0:T(8,128)S(1)}, u32[]{:S(2)}, u32[]{:S(2)}) collective-permute-start(f32[6,48,256]{2,1,0:T(8,128)S(1)} %collective-permute-done.9.refs_10_), channel_id=1, source_target_pairs={{0,14},{1,15},{2,0},{3,1},{4,2},{5,3},{6,4},{7,5},{8,6},{9,7},{10,... | collective-permute-start | bytes 884744 | tf_op jit(solution)/shard_map/ppermute | solution.py:22
  52.0 4.0 %collective-permute-done.11.refs_2_ = f32[6,48,256]{2,1,0:T(8,128)S(1)} collective-permute-done((f32[6,48,256]{2,1,0:T(8,128)S(1)}, f32[6,48,256]{2,1,0:T(8,128)S(1)}, u32[]{:S(2)}, u32[]{:S(2)}) %collective-permute-start.11) | collective-permute-done | bytes 294944 | tf_op jit(solution)/shard_map/ppermute | solution.py:22
  57.9 3.0 %collective-permute-start.25 = (f32[6,48,256]{2,1,0:T(8,128)S(1)}, f32[6,48,256]{2,1,0:T(8,128)S(1)}, u32[]{:S(2)}, u32[]{:S(2)}) collective-permute-start(f32[6,48,256]{2,1,0:T(8,128)S(1)} %broadcast_select_fusion), channel_id=1, source_target_pairs={{0,2},{1,15},{2,4},{3,1},{4,6},{5,3},{6,8},{7,5},{8,10},{9,7},{10,... | collective-permute-start | bytes 884744 | tf_op jit(solution)/shard_map/ppermute | solution.py:22
  60.9 4.3 %multiply.1 = (f32[2,48,768]{2,1,0:T(8,128)S(1)}, f32[2,48,768]{2,1,0:T(8,128)S(1)}, f32[2,48,768]{2,1,0:T(8,128)S(1)}, f32[2,48,768]{2,1,0:T(8,128)S(1)}, f32[2...) custom-call(s32[256]{0:T(256)S(1)} %copy-done, ...), custom_call_target="tpu_custom_call" | custom-call | flops 2717908992 | bytes 7077888 | tf_op jit(solution)/shard_map/multiply/pallas_call | solution.py:162
  65.9 2.2 %terms.1 = (f32[8,3,32,128]{3,2,1,0:T(8,128)S(1)}, f32[8,3,32,128]{3,2,1,0:T(8,128)S(1)}) custom-call(s32[3,48]{1,0:T(4,128)S(1)} %convert_element_type.18.listed_ref, f32[2,48,768]{2,1,0:T(8,128)S(1)} %get-tuple-element.48.refs_0_, f32[2,48,768]{2,1,0:T(8,128)S(1)} %get-tuple-element.49.refs_1_, f32[2,48,768]{2,1,0:T(8,128)S(1)} %get-tuple-element.50.refs_2_, ...), custom_call_target="tpu_custom_call" | custom-call | flops 905969664 | bytes 4718592 | tf_op jit(solution)/shard_map/terms/pallas_call | solution.py:213
  68.2 1.8 %collective-permute-start.17 = (f32[2,48,768]{2,1,0:T(8,128)S(1)}, f32[2,48,768]{2,1,0:T(8,128)S(1)}, u32[]{:S(2)}, u32[]{:S(2)}) collective-permute-start(f32[2,48,768]{2,1,0:T(8,128)S(1)} %get-tuple-element.52.refs_4_), channel_id=1, source_target_pairs={{0,2},{1,15},{2,4},{3,1},{4,6},{5,3},{6,8},{7,5},{8,10},{9,7},{10,... | collective-permute-start | bytes 884744 | tf_op jit(solution)/shard_map/ppermute | solution.py:22
  70.0 1.5 %collective-permute-start.21 = (f32[2,48,768]{2,1,0:T(8,128)S(1)}, f32[2,48,768]{2,1,0:T(8,128)S(1)}, u32[]{:S(2)}, u32[]{:S(2)}) collective-permute-start(f32[2,48,768]{2,1,0:T(8,128)S(1)} %get-tuple-element.55.refs_5_), channel_id=1, source_target_pairs={{0,14},{1,3},{2,0},{3,5},{4,2},{5,7},{6,4},{7,9},{8,6},{9,11},{10,... | collective-permute-start | bytes 884744 | tf_op jit(solution)/shard_map/ppermute | solution.py:22
  71.5 7.8 %collective-permute-done.17 = f32[2,48,768]{2,1,0:T(8,128)S(1)} collective-permute-done((f32[2,48,768]{2,1,0:T(8,128)S(1)}, f32[2,48,768]{2,1,0:T(8,128)S(1)}, u32[]{:S(2)}, u32[]{:S(2)}) %collective-permute-start.17) | collective-permute-done | bytes 294944 | tf_op jit(solution)/shard_map/ppermute | solution.py:22
  80.3 8.2 %all-to-all-start = ((f32[8,3,32,128]{3,2,1,0:T(8,128)}), f32[8,3,32,128]{3,2,1,0:T(8,128)S(1)}, u32[]{:S(2)}, u32[]{:S(2)}) async-start(f32[8,3,32,128]{3,2,1,0:T(8,128)} %add.97), calls=%async_computation | async-start | bytes 786432 | tf_op jit(solution)/shard_map/all_to_all | solution.py:292
  88.5 3.3 %collective-permute-start.22 = (f32[2,48,768]{2,1,0:T(8,128)S(1)}, f32[2,48,768]{2,1,0:T(8,128)S(1)}, u32[]{:S(2)}, u32[]{:S(2)}) collective-permute-start(f32[2,48,768]{2,1,0:T(8,128)S(1)} %add.88), channel_id=1, source_target_pairs={{0,14},{1,3},{2,0},{3,5},{4,2},{5,7},{6,4},{7,9},{8,6},{9,11},{10,... | collective-permute-start | bytes 884744 | tf_op jit(solution)/shard_map/ppermute | solution.py:22
  92.0 3.4 %all-to-all-done = f32[8,3,32,128]{3,2,1,0:T(8,128)S(1)} async-done(((f32[8,3,32,128]{3,2,1,0:T(8,128)}), f32[8,3,32,128]{3,2,1,0:T(8,128)S(1)}, u32[]{:S(2)}, u32[]{:S(2)}) %all-to-all-start) | async-done | bytes 393248 | tf_op jit(solution)/shard_map/all_to_all | solution.py:292
  95.3 1.9 %collective-permute-start.27 = (f32[3,32,128]{2,1,0:T(8,128)S(1)}, f32[3,32,128]{2,1,0:T(8,128)S(1)}, u32[]{:S(2)}, u32[]{:S(2)}) collective-permute-start(f32[3,32,128]{2,1,0:T(8,128)S(1)} %reduce_sum.9), channel_id=1, source_target_pairs={{0,16},{1,17},{2,18},{3,19},{4,20},{5,21},{6,22},{7,23},{8,24},{9,... | collective-permute-start | bytes 147464 | tf_op jit(solution)/shard_map/ppermute | solution.py:22
  97.3 2.3 %collective-permute-done.27 = f32[3,32,128]{2,1,0:T(8,128)S(1)} collective-permute-done((f32[3,32,128]{2,1,0:T(8,128)S(1)}, f32[3,32,128]{2,1,0:T(8,128)S(1)}, u32[]{:S(2)}, u32[]{:S(2)}) %collective-permute-start.27) | collective-permute-done | bytes 49184 | tf_op jit(solution)/shard_map/ppermute | solution.py:22
  100.5 3.2 %collective-permute-done.28 = f32[3,32,128]{2,1,0:T(8,128)S(1)} collective-permute-done((f32[3,32,128]{2,1,0:T(8,128)S(1)}, f32[3,32,128]{2,1,0:T(8,128)S(1)}, u32[]{:S(2)}, u32[]{:S(2)}) %collective-permute-start.28) | collective-permute-done | bytes 49184 | tf_op jit(solution)/shard_map/ppermute | solution.py:22
  103.7 2.4 %collective-permute-start.29 = (f32[3,32,128]{2,1,0:T(8,128)S(1)}, f32[3,32,128]{2,1,0:T(8,128)S(1)}, u32[]{:S(2)}, u32[]{:S(2)}) collective-permute-start(f32[3,32,128]{2,1,0:T(8,128)S(1)} %add.99), channel_id=1, source_target_pairs={{0,4},{1,5},{2,6},{3,15},{4,0},{5,1},{6,2},{7,11},{8,12},{9,13},{1... | collective-permute-start | bytes 147464 | tf_op jit(solution)/shard_map/ppermute | solution.py:22
  106.1 2.9 %collective-permute-done.29 = f32[3,32,128]{2,1,0:T(8,128)S(1)} collective-permute-done((f32[3,32,128]{2,1,0:T(8,128)S(1)}, f32[3,32,128]{2,1,0:T(8,128)S(1)}, u32[]{:S(2)}, u32[]{:S(2)}) %collective-permute-start.29) | collective-permute-done | bytes 49184 | tf_op jit(solution)/shard_map/ppermute | solution.py:22
  109.0 4.4 %collective-permute-start.30 = (f32[3,32,128]{2,1,0:T(8,128)S(1)}, f32[3,32,128]{2,1,0:T(8,128)S(1)}, u32[]{:S(2)}, u32[]{:S(2)}) collective-permute-start(f32[3,32,128]{2,1,0:T(8,128)S(1)} %add.100), channel_id=1, source_target_pairs={{0,8},{1,9},{2,10},{3,11},{4,12},{5,13},{6,14},{7,15},{8,0},{9,1},... | collective-permute-start | bytes 147464 | tf_op jit(solution)/shard_map/ppermute | solution.py:22
  113.5 1.9 %collective-permute-start.23 = (f32[2,48,768]{2,1,0:T(8,128)S(1)}, f32[2,48,768]{2,1,0:T(8,128)S(1)}, u32[]{:S(2)}, u32[]{:S(2)}) collective-permute-start(f32[2,48,768]{2,1,0:T(8,128)S(1)} %add.89), channel_id=1, source_target_pairs={{0,14},{1,3},{2,0},{3,5},{4,2},{5,7},{6,4},{7,9},{8,6},{9,11},{10,... | collective-permute-start | bytes 884744 | tf_op jit(solution)/shard_map/ppermute | solution.py:22
  115.7 1.5 %collective-permute-done.30 = f32[3,32,128]{2,1,0:T(8,128)S(1)} collective-permute-done((f32[3,32,128]{2,1,0:T(8,128)S(1)}, f32[3,32,128]{2,1,0:T(8,128)S(1)}, u32[]{:S(2)}, u32[]{:S(2)}) %collective-permute-start.30) | collective-permute-done | bytes 49184 | tf_op jit(solution)/shard_map/ppermute | solution.py:22
  118.6 2.9 %collective-permute-done.23 = f32[2,48,768]{2,1,0:T(8,128)S(1)} collective-permute-done((f32[2,48,768]{2,1,0:T(8,128)S(1)}, f32[2,48,768]{2,1,0:T(8,128)S(1)}, u32[]{:S(2)}, u32[]{:S(2)}) %collective-permute-start.23) | collective-permute-done | bytes 294944 | tf_op jit(solution)/shard_map/ppermute | solution.py:22
  121.5 1.9 %collective-permute-done.20 = f32[2,48,768]{2,1,0:T(8,128)S(1)} collective-permute-done((f32[2,48,768]{2,1,0:T(8,128)S(1)}, f32[2,48,768]{2,1,0:T(8,128)S(1)}, u32[]{:S(2)}, u32[]{:S(2)}) %collective-permute-start.20) | collective-permute-done | bytes 294944 | tf_op jit(solution)/shard_map/ppermute | solution.py:22
  123.5 2.1 %collective-permute-start.24 = (f32[48,768]{1,0:T(8,128)S(1)}, f32[48,768]{1,0:T(8,128)S(1)}, u32[]{:S(2)}, u32[]{:S(2)}) collective-permute-start(f32[48,768]{1,0:T(8,128)S(1)} %dynamic-slice_bitcast_fusion), channel_id=1, source_target_pairs={{0,16},{1,17},{2,18},{3,19},{4,20},{5,21},{6,22},{7,23},{8,24},{9,... | collective-permute-start | bytes 442376 | tf_op jit(solution)/shard_map/ppermute | solution.py:22
  126.3 2.5 %collective-permute-done.24 = f32[48,768]{1,0:T(8,128)S(1)} collective-permute-done((f32[48,768]{1,0:T(8,128)S(1)}, f32[48,768]{1,0:T(8,128)S(1)}, u32[]{:S(2)}, u32[]{:S(2)}) %collective-permute-start.24) | collective-permute-done | bytes 147488 | tf_op jit(solution)/shard_map/ppermute | solution.py:22
  (76 shorter events, 14.4 us)
Async XLA Ops:
  2.5 23.0 %collective-permute-start.2 = (f32[768,384]{1,0:T(8,128)S(1)}, f32[768,384]{1,0:T(8,128)S(1)}, u32[]{:S(2)}, u32[]{:S(2)}) collective-permute-start(f32[768,384]{1,0:T(8,128)S(1)} %bitcast.20), channel_id=1, source_target_pairs={{0,1},{1,0},{2,3},{3,2},{4,5},{5,4},{6,7},{7,6},{8,9},{9,8},{10,11... | collective-permute-start | bytes 3538952 | tf_op jit(solution)/shard_map/ppermute | solution.py:22
  2.6 22.9 %collective-permute-start = (f32[3,48,256]{2,1,0:T(8,128)}, f32[3,48,256]{2,1,0:T(8,128)}, u32[]{:S(2)}, u32[]{:S(2)}) collective-permute-start(f32[3,48,256]{2,1,0:T(8,128)} %param.7), channel_id=1, source_target_pairs={{0,161},{1,97},{2,128},{3,224},{4,96},{5,0},{6,193},{7,33},{8,1},{... | collective-permute-start | bytes 442376 | tf_op jit(solution)/shard_map/ppermute | solution.py:22
  8.2 17.2 %collective-permute-start.1 = (f32[3,48,256]{2,1,0:T(8,128)}, f32[3,48,256]{2,1,0:T(8,128)}, u32[]{:S(2)}, u32[]{:S(2)}) collective-permute-start(f32[3,48,256]{2,1,0:T(8,128)} %param.7), channel_id=1, source_target_pairs={{0,16},{1,17},{2,18},{3,19},{4,20},{5,21},{6,22},{7,23},{8,24},{9,... | collective-permute-start | bytes 442376 | tf_op jit(solution)/shard_map/ppermute | solution.py:22
  26.5 10.2 %collective-permute-start.4 = (f32[6,48,256]{2,1,0:T(8,128)S(1)}, f32[6,48,256]{2,1,0:T(8,128)S(1)}, u32[]{:S(2)}, u32[]{:S(2)}) collective-permute-start(f32[6,48,256]{2,1,0:T(8,128)S(1)} %pad_maximum_fusion.1.refs_8_), channel_id=1, source_target_pairs={{0,2},{1,3},{2,4},{3,5},{4,6},{5,7},{6,8},{7,9},{8,10},{9,11},{10,... | collective-permute-start | bytes 884744 | tf_op jit(solution)/shard_map/ppermute | solution.py:22
  26.6 10.1 %collective-permute-start.5 = (f32[6,48,256]{2,1,0:T(8,128)S(1)}, f32[6,48,256]{2,1,0:T(8,128)S(1)}, u32[]{:S(2)}, u32[]{:S(2)}) collective-permute-start(f32[6,48,256]{2,1,0:T(8,128)S(1)} %pad_maximum_fusion.1.refs_8_), channel_id=1, source_target_pairs={{0,14},{1,15},{2,0},{3,1},{4,2},{5,3},{6,4},{7,5},{8,6},{9,7},{10,... | collective-permute-start | bytes 884744 | tf_op jit(solution)/shard_map/ppermute | solution.py:22
  29.8 6.9 %collective-permute-start.3 = (f32[3,48,256]{2,1,0:T(8,128)}, f32[3,48,256]{2,1,0:T(8,128)S(1)}, u32[]{:S(2)}, u32[]{:S(2)}) collective-permute-start(f32[3,48,256]{2,1,0:T(8,128)} %collective-permute-done), channel_id=1, source_target_pairs={{0,32},{1,33},{2,34},{3,35},{4,36},{5,37},{6,38},{7,39},{8,40},{9,... | collective-permute-start | bytes 442376 | tf_op jit(solution)/shard_map/ppermute | solution.py:22
  36.7 8.0 %collective-permute-start.6 = (f32[6,48,256]{2,1,0:T(8,128)S(1)}, f32[6,48,256]{2,1,0:T(8,128)S(1)}, u32[]{:S(2)}, u32[]{:S(2)}) collective-permute-start(f32[6,48,256]{2,1,0:T(8,128)S(1)} %constant_dynamic-update-slice_fusion.refs_0_), channel_id=1, source_target_pairs={{0,64},{1,65},{2,66},{3,67},{4,68},{5,69},{6,70},{7,71},{8,72},{9,... | collective-permute-start | bytes 884744 | tf_op jit(solution)/shard_map/ppermute | solution.py:22
  36.8 7.9 %collective-permute-start.7 = (f32[6,48,256]{2,1,0:T(8,128)S(1)}, f32[6,48,256]{2,1,0:T(8,128)S(1)}, u32[]{:S(2)}, u32[]{:S(2)}) collective-permute-start(f32[6,48,256]{2,1,0:T(8,128)S(1)} %constant_dynamic-update-slice_fusion.refs_0_), channel_id=1, source_target_pairs={{0,192},{1,193},{2,194},{3,195},{4,196},{5,197},{6,198},{7,199},{8... | collective-permute-start | bytes 884744 | tf_op jit(solution)/shard_map/ppermute | solution.py:22
  40.0 7.9 %collective-permute-start.8 = (f32[6,48,256]{2,1,0:T(8,128)S(1)}, f32[6,48,256]{2,1,0:T(8,128)S(1)}, u32[]{:S(2)}, u32[]{:S(2)}) collective-permute-start(f32[6,48,256]{2,1,0:T(8,128)S(1)} %collective-permute-done.4.refs_15_), channel_id=1, source_target_pairs={{0,2},{1,3},{2,4},{3,5},{4,6},{5,7},{6,8},{7,9},{8,10},{9,11},{10,... | collective-permute-start | bytes 884744 | tf_op jit(solution)/shard_map/ppermute | solution.py:22
  40.0 7.9 %collective-permute-start.9 = (f32[6,48,256]{2,1,0:T(8,128)S(1)}, f32[6,48,256]{2,1,0:T(8,128)S(1)}, u32[]{:S(2)}, u32[]{:S(2)}) collective-permute-start(f32[6,48,256]{2,1,0:T(8,128)S(1)} %collective-permute-done.5.refs_9_), channel_id=1, source_target_pairs={{0,14},{1,15},{2,0},{3,1},{4,2},{5,3},{6,4},{7,5},{8,6},{9,7},{10,... | collective-permute-start | bytes 884744 | tf_op jit(solution)/shard_map/ppermute | solution.py:22
  43.3 4.7 %collective-permute-start.10 = (f32[6,48,256]{2,1,0:T(8,128)S(1)}, f32[6,48,256]{2,1,0:T(8,128)S(1)}, u32[]{:S(2)}, u32[]{:S(2)}) collective-permute-start(f32[6,48,256]{2,1,0:T(8,128)S(1)} %constant_dynamic-update-slice_fusion.refs_0_), channel_id=1, source_target_pairs={{0,1},{1,0},{2,3},{3,2},{4,5},{5,4},{6,7},{7,6},{8,9},{9,8},{10,11... | collective-permute-start | bytes 884744 | tf_op jit(solution)/shard_map/ppermute | solution.py:22
  48.0 8.0 %collective-permute-start.11 = (f32[6,48,256]{2,1,0:T(8,128)S(1)}, f32[6,48,256]{2,1,0:T(8,128)S(1)}, u32[]{:S(2)}, u32[]{:S(2)}) collective-permute-start(f32[6,48,256]{2,1,0:T(8,128)S(1)} %broadcast_select_fusion.1), channel_id=1, source_target_pairs={{0,64},{1,193},{2,66},{3,195},{4,68},{5,197},{6,70},{7,199},{8,72}... | collective-permute-start | bytes 884744 | tf_op jit(solution)/shard_map/ppermute | solution.py:22
  48.1 8.7 %collective-permute-start.12 = (f32[6,48,256]{2,1,0:T(8,128)S(1)}, f32[6,48,256]{2,1,0:T(8,128)S(1)}, u32[]{:S(2)}, u32[]{:S(2)}) collective-permute-start(f32[6,48,256]{2,1,0:T(8,128)S(1)} %collective-permute-done.8.refs_14_), channel_id=1, source_target_pairs={{0,2},{1,3},{2,4},{3,5},{4,6},{5,7},{6,8},{7,9},{8,10},{9,11},{10,... | collective-permute-start | bytes 884744 | tf_op jit(solution)/shard_map/ppermute | solution.py:22
  49.9 8.0 %collective-permute-start.13 = (f32[6,48,256]{2,1,0:T(8,128)S(1)}, f32[6,48,256]{2,1,0:T(8,128)S(1)}, u32[]{:S(2)}, u32[]{:S(2)}) collective-permute-start(f32[6,48,256]{2,1,0:T(8,128)S(1)} %collective-permute-done.9.refs_10_), channel_id=1, source_target_pairs={{0,14},{1,15},{2,0},{3,1},{4,2},{5,3},{6,4},{7,5},{8,6},{9,7},{10,... | collective-permute-start | bytes 884744 | tf_op jit(solution)/shard_map/ppermute | solution.py:22
  51.5 6.3 %collective-permute-start.14 = (f32[6,48,256]{2,1,0:T(8,128)S(1)}, f32[6,48,256]{2,1,0:T(8,128)S(1)}, u32[]{:S(2)}, u32[]{:S(2)}) collective-permute-start(f32[6,48,256]{2,1,0:T(8,128)S(1)} %collective-permute-done.6.refs_3_), channel_id=1, source_target_pairs={{0,1},{1,0},{2,3},{3,2},{4,5},{5,4},{6,7},{7,6},{8,9},{9,8},{10,11... | collective-permute-start | bytes 884744 | tf_op jit(solution)/shard_map/ppermute | solution.py:22
  51.5 6.3 %collective-permute-start.15 = (f32[6,48,256]{2,1,0:T(8,128)S(1)}, f32[6,48,256]{2,1,0:T(8,128)S(1)}, u32[]{:S(2)}, u32[]{:S(2)}) collective-permute-start(f32[6,48,256]{2,1,0:T(8,128)S(1)} %collective-permute-done.7.refs_1_), channel_id=1, source_target_pairs={{0,1},{1,0},{2,3},{3,2},{4,5},{5,4},{6,7},{7,6},{8,9},{9,8},{10,11... | collective-permute-start | bytes 884744 | tf_op jit(solution)/shard_map/ppermute | solution.py:22
  57.8 3.1 %collective-permute-start.16 = (f32[6,48,256]{2,1,0:T(8,128)S(1)}, f32[6,48,256]{2,1,0:T(8,128)S(1)}, u32[]{:S(2)}, u32[]{:S(2)}) collective-permute-start(f32[6,48,256]{2,1,0:T(8,128)S(1)} %collective-permute-done.11.refs_2_), channel_id=1, source_target_pairs={{0,1},{1,0},{2,3},{3,2},{4,5},{5,4},{6,7},{7,6},{8,9},{9,8},{10,11... | collective-permute-start | bytes 884744 | tf_op jit(solution)/shard_map/ppermute | solution.py:22
  57.9 8.0 %collective-permute-start.25 = (f32[6,48,256]{2,1,0:T(8,128)S(1)}, f32[6,48,256]{2,1,0:T(8,128)S(1)}, u32[]{:S(2)}, u32[]{:S(2)}) collective-permute-start(f32[6,48,256]{2,1,0:T(8,128)S(1)} %broadcast_select_fusion), channel_id=1, source_target_pairs={{0,2},{1,15},{2,4},{3,1},{4,6},{5,3},{6,8},{7,5},{8,10},{9,7},{10,... | collective-permute-start | bytes 884744 | tf_op jit(solution)/shard_map/ppermute | solution.py:22
  68.0 11.4 %collective-permute-start.26 = (f32[8,3,32,128]{3,2,1,0:T(8,128)S(1)}, f32[8,3,32,128]{3,2,1,0:T(8,128)S(1)}, u32[]{:S(2)}, u32[]{:S(2)}) collective-permute-start(f32[8,3,32,128]{3,2,1,0:T(8,128)S(1)} %get-tuple-element.59), channel_id=1, source_target_pairs={{0,1},{1,0},{2,3},{3,2},{4,5},{5,4},{6,7},{7,6},{8,9},{9,8},{10,11... | collective-permute-start | bytes 1179656 | tf_op jit(solution)/shard_map/ppermute | solution.py:22
  68.2 11.2 %collective-permute-start.17 = (f32[2,48,768]{2,1,0:T(8,128)S(1)}, f32[2,48,768]{2,1,0:T(8,128)S(1)}, u32[]{:S(2)}, u32[]{:S(2)}) collective-permute-start(f32[2,48,768]{2,1,0:T(8,128)S(1)} %get-tuple-element.52.refs_4_), channel_id=1, source_target_pairs={{0,2},{1,15},{2,4},{3,1},{4,6},{5,3},{6,8},{7,5},{8,10},{9,7},{10,... | collective-permute-start | bytes 884744 | tf_op jit(solution)/shard_map/ppermute | solution.py:22
  70.0 18.5 %collective-permute-start.21 = (f32[2,48,768]{2,1,0:T(8,128)S(1)}, f32[2,48,768]{2,1,0:T(8,128)S(1)}, u32[]{:S(2)}, u32[]{:S(2)}) collective-permute-start(f32[2,48,768]{2,1,0:T(8,128)S(1)} %get-tuple-element.55.refs_5_), channel_id=1, source_target_pairs={{0,14},{1,3},{2,0},{3,5},{4,2},{5,7},{6,4},{7,9},{8,6},{9,11},{10,... | collective-permute-start | bytes 884744 | tf_op jit(solution)/shard_map/ppermute | solution.py:22
  79.3 12.5 %collective-permute-start.18 = (f32[2,48,768]{2,1,0:T(8,128)S(1)}, f32[2,48,768]{2,1,0:T(8,128)S(1)}, u32[]{:S(2)}, u32[]{:S(2)}) collective-permute-start(f32[2,48,768]{2,1,0:T(8,128)S(1)} %add.84), channel_id=1, source_target_pairs={{0,2},{1,15},{2,4},{3,1},{4,6},{5,3},{6,8},{7,5},{8,10},{9,7},{10,... | collective-permute-start | bytes 884744 | tf_op jit(solution)/shard_map/ppermute | solution.py:22
  80.3 15.1 %all-to-all-start = ((f32[8,3,32,128]{3,2,1,0:T(8,128)}), f32[8,3,32,128]{3,2,1,0:T(8,128)S(1)}, u32[]{:S(2)}, u32[]{:S(2)}) async-start(f32[8,3,32,128]{3,2,1,0:T(8,128)} %add.97), calls=%async_computation | async-start | bytes 786432 | tf_op jit(solution)/shard_map/all_to_all | solution.py:292
  88.5 24.9 %collective-permute-start.22 = (f32[2,48,768]{2,1,0:T(8,128)S(1)}, f32[2,48,768]{2,1,0:T(8,128)S(1)}, u32[]{:S(2)}, u32[]{:S(2)}) collective-permute-start(f32[2,48,768]{2,1,0:T(8,128)S(1)} %add.88), channel_id=1, source_target_pairs={{0,14},{1,3},{2,0},{3,5},{4,2},{5,7},{6,4},{7,9},{8,6},{9,11},{10,... | collective-permute-start | bytes 884744 | tf_op jit(solution)/shard_map/ppermute | solution.py:22
  91.9 23.5 %collective-permute-start.19 = (f32[2,48,768]{2,1,0:T(8,128)S(1)}, f32[2,48,768]{2,1,0:T(8,128)S(1)}, u32[]{:S(2)}, u32[]{:S(2)}) collective-permute-start(f32[2,48,768]{2,1,0:T(8,128)S(1)} %add.85), channel_id=1, source_target_pairs={{0,2},{1,15},{2,4},{3,1},{4,6},{5,3},{6,8},{7,5},{8,10},{9,7},{10,... | collective-permute-start | bytes 884744 | tf_op jit(solution)/shard_map/ppermute | solution.py:22
  95.3 4.2 %collective-permute-start.27 = (f32[3,32,128]{2,1,0:T(8,128)S(1)}, f32[3,32,128]{2,1,0:T(8,128)S(1)}, u32[]{:S(2)}, u32[]{:S(2)}) collective-permute-start(f32[3,32,128]{2,1,0:T(8,128)S(1)} %reduce_sum.9), channel_id=1, source_target_pairs={{0,16},{1,17},{2,18},{3,19},{4,20},{5,21},{6,22},{7,23},{8,24},{9,... | collective-permute-start | bytes 147464 | tf_op jit(solution)/shard_map/ppermute | solution.py:22
  99.5 4.2 %collective-permute-start.28 = (f32[3,32,128]{2,1,0:T(8,128)S(1)}, f32[3,32,128]{2,1,0:T(8,128)S(1)}, u32[]{:S(2)}, u32[]{:S(2)}) collective-permute-start(f32[3,32,128]{2,1,0:T(8,128)S(1)} %add.98), channel_id=1, source_target_pairs={{0,2},{1,15},{2,0},{3,5},{4,6},{5,3},{6,4},{7,9},{8,10},{9,7},{10,... | collective-permute-start | bytes 147464 | tf_op jit(solution)/shard_map/ppermute | solution.py:22
  103.7 5.3 %collective-permute-start.29 = (f32[3,32,128]{2,1,0:T(8,128)S(1)}, f32[3,32,128]{2,1,0:T(8,128)S(1)}, u32[]{:S(2)}, u32[]{:S(2)}) collective-permute-start(f32[3,32,128]{2,1,0:T(8,128)S(1)} %add.99), channel_id=1, source_target_pairs={{0,4},{1,5},{2,6},{3,15},{4,0},{5,1},{6,2},{7,11},{8,12},{9,13},{1... | collective-permute-start | bytes 147464 | tf_op jit(solution)/shard_map/ppermute | solution.py:22
  109.0 8.2 %collective-permute-start.30 = (f32[3,32,128]{2,1,0:T(8,128)S(1)}, f32[3,32,128]{2,1,0:T(8,128)S(1)}, u32[]{:S(2)}, u32[]{:S(2)}) collective-permute-start(f32[3,32,128]{2,1,0:T(8,128)S(1)} %add.100), channel_id=1, source_target_pairs={{0,8},{1,9},{2,10},{3,11},{4,12},{5,13},{6,14},{7,15},{8,0},{9,1},... | collective-permute-start | bytes 147464 | tf_op jit(solution)/shard_map/ppermute | solution.py:22
  113.5 8.0 %collective-permute-start.23 = (f32[2,48,768]{2,1,0:T(8,128)S(1)}, f32[2,48,768]{2,1,0:T(8,128)S(1)}, u32[]{:S(2)}, u32[]{:S(2)}) collective-permute-start(f32[2,48,768]{2,1,0:T(8,128)S(1)} %add.89), channel_id=1, source_target_pairs={{0,14},{1,3},{2,0},{3,5},{4,2},{5,7},{6,4},{7,9},{8,6},{9,11},{10,... | collective-permute-start | bytes 884744 | tf_op jit(solution)/shard_map/ppermute | solution.py:22
  115.5 8.0 %collective-permute-start.20 = (f32[2,48,768]{2,1,0:T(8,128)S(1)}, f32[2,48,768]{2,1,0:T(8,128)S(1)}, u32[]{:S(2)}, u32[]{:S(2)}) collective-permute-start(f32[2,48,768]{2,1,0:T(8,128)S(1)} %add.86), channel_id=1, source_target_pairs={{0,2},{1,15},{2,4},{3,1},{4,6},{5,3},{6,8},{7,5},{8,10},{9,7},{10,... | collective-permute-start | bytes 884744 | tf_op jit(solution)/shard_map/ppermute | solution.py:22
  123.5 5.2 %collective-permute-start.24 = (f32[48,768]{1,0:T(8,128)S(1)}, f32[48,768]{1,0:T(8,128)S(1)}, u32[]{:S(2)}, u32[]{:S(2)}) collective-permute-start(f32[48,768]{1,0:T(8,128)S(1)} %dynamic-slice_bitcast_fusion), channel_id=1, source_target_pairs={{0,16},{1,17},{2,18},{3,19},{4,20},{5,21},{6,22},{7,23},{8,24},{9,... | collective-permute-start | bytes 442376 | tf_op jit(solution)/shard_map/ppermute | solution.py:22
  (5 other events, 57.1 us)

commit v3 on v2

--- a/solution.py
+++ b/solution.py
@@ -52,6 +52,10 @@
 
 def z_pair(bit):
     return lambda y, xh, xl, z, c: (y, xh, xl, (((z + c) % 8 ^ bit) - c) % 8, c)
+
+
+def other_xl_and_z_pair(y, xh, xl, z, c):
+    return z_pair(1)(y, xh, 1 - xl, z, c)
 
 
 SHARES = (
@@ -242,7 +246,7 @@
     halves = inverse_block.reshape(16, 2, rows, span)
     s_own, s_give = pick(halves, core, 1), pick(halves, 1 - core, 1)
     s_own, s_other = s_own.reshape(16 * rows, span), facing(s_give.reshape(16 * rows, span))
-    share, beside, s_other = both(share, beside, s_other)
+    share, s_other = both(share, s_other)
 
     near = send(share, other_xh)
     line = jnp.concatenate(
@@ -255,22 +259,18 @@
     s_high, s_low = split(s_chip)
     listed = listed_blocks(block_lists, list_counts, jnp.arange(block_lists.shape[1], dtype=jnp.int32))
     listed = listed.astype(jnp.int32)
-    near, line_down, line_up, s_high, s_low, listed = both(near, line_down, line_up, s_high, s_low, listed)
+    near, s_high, s_low, listed = both(near, s_high, s_low, listed)
 
     pair = jnp.concatenate([share, near])
     below, above = send(pair, y_by(lambda c: 1)), send(pair, y_by(lambda c: -1))
     line_down2, line_up2 = send(line_down, z_by(lambda c: 1)), send(line_up, z_by(lambda c: -1))
     pair_facing = facing(pair)
-    below, above, line_down2, line_up2, pair_facing = both(below, above, line_down2, line_up2, pair_facing)
-
     far = send(jnp.where(core == 0, below, above), y_by(lambda c: 1 - 2 * c))
     line_down3, line_up3 = send(line_down2, z_by(lambda c: 1)), send(line_up2, z_by(lambda c: -1))
     below_facing, above_facing = facing(below), facing(above)
-    far, line_down3, line_up3, below_facing, above_facing = both(
-        far, line_down3, line_up3, below_facing, above_facing
-    )
+    far_facing = facing(far)
     line_far = send(jnp.where(core == 0, line_down3, line_up3), z_by(lambda c: 1 - 2 * c))
-    pieces = [pair, above, far, below, pair_facing, above_facing, facing(far), below_facing]
+    pieces = [pair, above, far, below, pair_facing, above_facing, far_facing, below_facing]
     chunks = multiply(listed, s_high, s_low, pieces)
 
     first = send(chunks[4], z_by(ahead))
@@ -291,10 +291,10 @@
     terms = keep + facing(give)
     terms = lax.all_to_all(terms, "row", 0, 0, tiled=True)
     terms = jnp.sum(terms, axis=0)
-    terms = terms + send(terms, other_xl)
-    terms = terms + send(terms, z_pair(1))
-    terms = terms + send(terms, z_pair(2))
-    terms = terms + send(terms, z_pair(4))
+    there, across, past = send(terms, z_pair(1)), send(terms, other_xl), send(terms, other_xl_and_z_pair)
+    terms = (terms + there) + (across + past)
+    there, over, under = (send(terms, z_by(lambda c, k=k: k)) for k in (4, 2, -2))
+    terms = (terms + there) + (over + under)
     rest = facing(terms)
     diag_block = diag_inverse + jnp.concatenate(
         [jnp.where(core == 0, terms, rest), jnp.where(core == 0, rest, terms)], axis=2

time: 132 us -> 121 us (0.917); the launches traced: 130 us -> 120 us
  waiting for transfers between devices: 61.8 us -> 45.7 us
  starting transfers between devices: 53.1 us -> 60.8 us
    ppermute x32 -> x34, waiting for transfers between devices: 58.5 us -> 40 us  [send(): return lax.ppermute(array, AXES, pairs)]
    ppermute x32 -> x34, starting transfers between devices: 44.8 us -> 53.6 us  [send(): return lax.ppermute(array, AXES, pairs)]
    all_to_all x1, waiting for transfers between devices: 3.36 us -> 5.67 us  [per_device(): terms = lax.all_to_all(terms, 'row', 0, 0, tiled=True)]
  transfers between devices with their start and end apart: 33 -> 35, of which waited for: 18 -> 18; matrix products, arithmetic and copies ran while one was open for 3% -> 2% of each run, Pallas kernels for 3% -> 4%
where the time goes in v3:
time: 121 us; the launch traced here: 120 us
  starting transfers between devices  60.8 us (50%)
  waiting for transfers between devices  45.7 us (38%)
  Pallas kernels  6.38 us (5%)
  other arithmetic  3.5 us (3%)
  local copies, waits for them, and re-layouts  2.94 us (2%)
    ppermute x34, starting transfers between devices, send(): return lax.ppermute(array, AXES, pairs)  53.6 us
    ppermute x34, waiting for transfers between devices, send(): return lax.ppermute(array, AXES, pairs)  40 us
    all_to_all x1, starting transfers between devices, per_device(): terms = lax.all_to_all(terms, 'row', 0, 0, tiled=True)  7.18 us
    all_to_all x1, waiting for transfers between devices, per_device(): terms = lax.all_to_all(terms, 'row', 0, 0, tiled=True)  5.67 us
    pallas_call x1, Pallas kernels, multiply(): pl.pallas_call(multiply_kernel, out_shape=[jax.ShapeDtypeStruct((2, rows,...  4.27 us
    dynamic_slice x1, local copies, waits for them, and re-layouts, pick(): return lax.dynamic_index_in_dim(array, index, axis, keepdims=False)  2.86 us
  transfers between devices with their start and end apart: 35, of which 18 were waited for; matrix products, arithmetic and copies ran while one was open for 2% of the time, Pallas kernels for 4%

profile of v3, /device:TPU:6, one launch (start us, length us, event | category | flops | bytes accessed | tf_op | source)
XLA Modules:
  0.0 120.3 jit_solution(12833813716656240498)
XLA Ops:
  0.7 2.9 %constant_dynamic-slice_fusion = (f32[16,1,48,384]{3,2,1,0:T(8,128)S(1)}, f32[16,1,48,384]{3,2,1,0:T(8,128)}) fusion(f32[16,2,48,384]{3,2,1,0:T(8,128)} %bitcast.19, s32[]{:T(128)S(6)} %select_n.85, s32[]{:T(128)S(6)} %select_n.83), kind=kLoop, calls=%fused_computation.35 | loop fusion | bytes 4718600 | tf_op jit(solution)/shard_map/jit(dynamic_index_in_dim)/dynamic_slice | solution.py:106
  4.5 6.0 %collective-permute-start = (f32[3,48,256]{2,1,0:T(8,128)S(1)}, f32[3,48,256]{2,1,0:T(8,128)S(1)}, u32[]{:S(2)}, u32[]{:S(2)}) collective-permute-start(f32[3,48,256]{2,1,0:T(8,128)S(1)} %copy-done.1), channel_id=1, source_target_pairs={{0,161},{1,97},{2,128},{3,224},{4,96},{5,0},{6,193},{7,33},{8,1},{... | collective-permute-start | bytes 442376 | tf_op jit(solution)/shard_map/ppermute | solution.py:22
  10.5 5.3 %collective-permute-start.19 = (f32[6,48,256]{2,1,0:T(8,128)S(1)}, f32[6,48,256]{2,1,0:T(8,128)S(1)}, u32[]{:S(2)}, u32[]{:S(2)}) collective-permute-start(f32[6,48,256]{2,1,0:T(8,128)S(1)} %pad_maximum_fusion.1.refs_8_), channel_id=1, source_target_pairs={{0,14},{1,15},{2,0},{3,1},{4,2},{5,3},{6,4},{7,5},{8,6},{9,7},{10,... | collective-permute-start | bytes 884744 | tf_op jit(solution)/shard_map/ppermute | solution.py:22
  16.2 5.5 %collective-permute-done.19.refs_9_ = f32[6,48,256]{2,1,0:T(8,128)S(1)} collective-permute-done((f32[6,48,256]{2,1,0:T(8,128)S(1)}, f32[6,48,256]{2,1,0:T(8,128)S(1)}, u32[]{:S(2)}, u32[]{:S(2)}) %collective-permute-start.19) | collective-permute-done | bytes 294944 | tf_op jit(solution)/shard_map/ppermute | solution.py:22
  21.8 3.7 %collective-permute-start.20 = (f32[6,48,256]{2,1,0:T(8,128)S(1)}, f32[6,48,256]{2,1,0:T(8,128)S(1)}, u32[]{:S(2)}, u32[]{:S(2)}) collective-permute-start(f32[6,48,256]{2,1,0:T(8,128)S(1)} %collective-permute-done.19.refs_9_), channel_id=1, source_target_pairs={{0,14},{1,15},{2,0},{3,1},{4,2},{5,3},{6,4},{7,5},{8,6},{9,7},{10,... | collective-permute-start | bytes 884744 | tf_op jit(solution)/shard_map/ppermute | solution.py:22
  26.5 2.7 %collective-permute-start.2 = (f32[3,48,256]{2,1,0:T(8,128)S(1)}, f32[3,48,256]{2,1,0:T(8,128)S(1)}, u32[]{:S(2)}, u32[]{:S(2)}) collective-permute-start(f32[3,48,256]{2,1,0:T(8,128)S(1)} %collective-permute-done), channel_id=1, source_target_pairs={{0,32},{1,33},{2,34},{3,35},{4,36},{5,37},{6,38},{7,39},{8,40},{9,... | collective-permute-start | bytes 442376 | tf_op jit(solution)/shard_map/ppermute | solution.py:22
  29.7 3.4 %collective-permute-done.2 = f32[3,48,256]{2,1,0:T(8,128)S(1)} collective-permute-done((f32[3,48,256]{2,1,0:T(8,128)S(1)}, f32[3,48,256]{2,1,0:T(8,128)S(1)}, u32[]{:S(2)}, u32[]{:S(2)}) %collective-permute-start.2) | collective-permute-done | bytes 147488 | tf_op jit(solution)/shard_map/ppermute | solution.py:22
  33.2 10.3 %collective-permute-start.3 = (f32[6,48,256]{2,1,0:T(8,128)S(1)}, f32[6,48,256]{2,1,0:T(8,128)S(1)}, u32[]{:S(2)}, u32[]{:S(2)}) collective-permute-start(f32[6,48,256]{2,1,0:T(8,128)S(1)} %constant_dynamic-update-slice_fusion.refs_0_), channel_id=1, source_target_pairs={{0,192},{1,193},{2,194},{3,195},{4,196},{5,197},{6,198},{7,199},{8... | collective-permute-start | bytes 884744 | tf_op jit(solution)/shard_map/ppermute | solution.py:22
  43.4 3.2 %collective-permute-start.21 = (f32[6,48,256]{2,1,0:T(8,128)S(1)}, f32[6,48,256]{2,1,0:T(8,128)S(1)}, u32[]{:S(2)}, u32[]{:S(2)}) collective-permute-start(f32[6,48,256]{2,1,0:T(8,128)S(1)} %collective-permute-done.20.refs_10_), channel_id=1, source_target_pairs={{0,14},{1,15},{2,0},{3,1},{4,2},{5,3},{6,4},{7,5},{8,6},{9,7},{10,... | collective-permute-start | bytes 884744 | tf_op jit(solution)/shard_map/ppermute | solution.py:22
  46.7 2.3 %collective-permute-done.3.refs_1_ = f32[6,48,256]{2,1,0:T(8,128)S(1)} collective-permute-done((f32[6,48,256]{2,1,0:T(8,128)S(1)}, f32[6,48,256]{2,1,0:T(8,128)S(1)}, u32[]{:S(2)}, u32[]{:S(2)}) %collective-permute-start.3) | collective-permute-done | bytes 294944 | tf_op jit(solution)/shard_map/ppermute | solution.py:22
  49.0 2.3 %collective-permute-done.4.refs_3_ = f32[6,48,256]{2,1,0:T(8,128)S(1)} collective-permute-done((f32[6,48,256]{2,1,0:T(8,128)S(1)}, f32[6,48,256]{2,1,0:T(8,128)S(1)}, u32[]{:S(2)}, u32[]{:S(2)}) %collective-permute-start.4) | collective-permute-done | bytes 294944 | tf_op jit(solution)/shard_map/ppermute | solution.py:22
  52.3 7.1 %collective-permute-done.5.refs_2_ = f32[6,48,256]{2,1,0:T(8,128)S(1)} collective-permute-done((f32[6,48,256]{2,1,0:T(8,128)S(1)}, f32[6,48,256]{2,1,0:T(8,128)S(1)}, u32[]{:S(2)}, u32[]{:S(2)}) %collective-permute-start.5) | collective-permute-done | bytes 294944 | tf_op jit(solution)/shard_map/ppermute | solution.py:22
  59.9 1.1 collective-permute-done.8.refs_6_
  61.0 4.3 %multiply.1 = (f32[2,48,768]{2,1,0:T(8,128)S(1)}, f32[2,48,768]{2,1,0:T(8,128)S(1)}, f32[2,48,768]{2,1,0:T(8,128)S(1)}, f32[2,48,768]{2,1,0:T(8,128)S(1)}, f32[2...) custom-call(s32[256]{0:T(256)S(1)} %copy-done, ...), custom_call_target="tpu_custom_call" | custom-call | flops 2717908992 | bytes 7077888 | tf_op jit(solution)/shard_map/multiply/pallas_call | solution.py:166
  65.3 2.5 %collective-permute-done.25.refs_12_ = f32[6,48,256]{2,1,0:T(8,128)S(1)} collective-permute-done((f32[6,48,256]{2,1,0:T(8,128)S(1)}, f32[6,48,256]{2,1,0:T(8,128)S(1)}, u32[]{:S(2)}, u32[]{:S(2)}) %collective-permute-start.25) | collective-permute-done | bytes 294944 | tf_op jit(solution)/shard_map/ppermute | solution.py:22
  67.8 2.1 %terms.1 = (f32[8,3,32,128]{3,2,1,0:T(8,128)S(1)}, f32[8,3,32,128]{3,2,1,0:T(8,128)S(1)}) custom-call(s32[3,48]{1,0:T(4,128)S(1)} %convert_element_type.18.listed_ref, f32[2,48,768]{2,1,0:T(8,128)S(1)} %get-tuple-element.24.refs_0_, f32[2,48,768]{2,1,0:T(8,128)S(1)} %get-tuple-element.25.refs_1_, f32[2,48,768]{2,1,0:T(8,128)S(1)} %get-tuple-element.26.refs_2_, ...), custom_call_target="tpu_custom_call" | custom-call | flops 905969664 | bytes 4718592 | tf_op jit(solution)/shard_map/terms/pallas_call | solution.py:217
  70.1 1.6 %collective-permute-done.26 = f32[8,3,32,128]{3,2,1,0:T(8,128)S(1)} collective-permute-done((f32[8,3,32,128]{3,2,1,0:T(8,128)S(1)}, f32[8,3,32,128]{3,2,1,0:T(8,128)S(1)}, u32[]{:S(2)}, u32[]{:S(2)}) %collective-permute-start.26) | collective-permute-done | bytes 393248 | tf_op jit(solution)/shard_map/ppermute | solution.py:22
  72.5 7.2 %all-to-all-start = ((f32[8,3,32,128]{3,2,1,0:T(8,128)}), f32[8,3,32,128]{3,2,1,0:T(8,128)S(1)}, u32[]{:S(2)}, u32[]{:S(2)}) async-start(f32[8,3,32,128]{3,2,1,0:T(8,128)} %add.103), calls=%async_computation | async-start | bytes 786432 | tf_op jit(solution)/shard_map/all_to_all | solution.py:292
  79.7 1.6 %collective-permute-start.14 = (f32[2,48,768]{2,1,0:T(8,128)S(1)}, f32[2,48,768]{2,1,0:T(8,128)S(1)}, u32[]{:S(2)}, u32[]{:S(2)}) collective-permute-start(f32[2,48,768]{2,1,0:T(8,128)S(1)} %get-tuple-element.31.refs_5_), channel_id=1, source_target_pairs={{0,14},{1,3},{2,0},{3,5},{4,2},{5,7},{6,4},{7,9},{8,6},{9,11},{10,... | collective-permute-start | bytes 884744 | tf_op jit(solution)/shard_map/ppermute | solution.py:22
  81.8 5.7 %all-to-all-done = f32[8,3,32,128]{3,2,1,0:T(8,128)S(1)} async-done(((f32[8,3,32,128]{3,2,1,0:T(8,128)}), f32[8,3,32,128]{3,2,1,0:T(8,128)S(1)}, u32[]{:S(2)}, u32[]{:S(2)}) %all-to-all-start) | async-done | bytes 393248 | tf_op jit(solution)/shard_map/all_to_all | solution.py:292
  87.6 1.3 %collective-permute-start.28 = (f32[3,32,128]{2,1,0:T(8,128)S(1)}, f32[3,32,128]{2,1,0:T(8,128)S(1)}, u32[]{:S(2)}, u32[]{:S(2)}) collective-permute-start(f32[3,32,128]{2,1,0:T(8,128)S(1)} %reduce_sum.9), channel_id=1, source_target_pairs={{0,16},{1,17},{2,18},{3,19},{4,20},{5,21},{6,22},{7,23},{8,24},{9,... | collective-permute-start | bytes 147464 | tf_op jit(solution)/shard_map/ppermute | solution.py:22
  88.9 2.2 %collective-permute-start.29 = (f32[3,32,128]{2,1,0:T(8,128)S(1)}, f32[3,32,128]{2,1,0:T(8,128)S(1)}, u32[]{:S(2)}, u32[]{:S(2)}) collective-permute-start(f32[3,32,128]{2,1,0:T(8,128)S(1)} %reduce_sum.9), channel_id=1, source_target_pairs={{0,18},{1,31},{2,16},{3,21},{4,22},{5,19},{6,20},{7,25},{8,26},{9,... | collective-permute-start | bytes 147464 | tf_op jit(solution)/shard_map/ppermute | solution.py:22
  91.1 1.3 %collective-permute-start.15 = (f32[2,48,768]{2,1,0:T(8,128)S(1)}, f32[2,48,768]{2,1,0:T(8,128)S(1)}, u32[]{:S(2)}, u32[]{:S(2)}) collective-permute-start(f32[2,48,768]{2,1,0:T(8,128)S(1)} %add.94), channel_id=1, source_target_pairs={{0,14},{1,3},{2,0},{3,5},{4,2},{5,7},{6,4},{7,9},{8,6},{9,11},{10,... | collective-permute-start | bytes 884744 | tf_op jit(solution)/shard_map/ppermute | solution.py:22
  94.0 3.3 %collective-permute-start.30 = (f32[3,32,128]{2,1,0:T(8,128)S(1)}, f32[3,32,128]{2,1,0:T(8,128)S(1)}, u32[]{:S(2)}, u32[]{:S(2)}) collective-permute-start(f32[3,32,128]{2,1,0:T(8,128)S(1)} %add_add_fusion.2), channel_id=1, source_target_pairs={{0,8},{1,9},{2,10},{3,11},{4,12},{5,13},{6,14},{7,15},{8,0},{9,1},... | collective-permute-start | bytes 147464 | tf_op jit(solution)/shard_map/ppermute | solution.py:22
  97.3 1.2 %collective-permute-start.31 = (f32[3,32,128]{2,1,0:T(8,128)S(1)}, f32[3,32,128]{2,1,0:T(8,128)S(1)}, u32[]{:S(2)}, u32[]{:S(2)}) collective-permute-start(f32[3,32,128]{2,1,0:T(8,128)S(1)} %add_add_fusion.2), channel_id=1, source_target_pairs={{0,4},{1,5},{2,6},{3,7},{4,8},{5,9},{6,10},{7,11},{8,12},{9,13},{1... | collective-permute-start | bytes 147464 | tf_op jit(solution)/shard_map/ppermute | solution.py:22
  98.6 2.9 %collective-permute-start.32 = (f32[3,32,128]{2,1,0:T(8,128)S(1)}, f32[3,32,128]{2,1,0:T(8,128)S(1)}, u32[]{:S(2)}, u32[]{:S(2)}) collective-permute-start(f32[3,32,128]{2,1,0:T(8,128)S(1)} %add_add_fusion.2), channel_id=1, source_target_pairs={{0,12},{1,13},{2,14},{3,15},{4,0},{5,1},{6,2},{7,3},{8,4},{9,5},{1... | collective-permute-start | bytes 147464 | tf_op jit(solution)/shard_map/ppermute | solution.py:22
  102.3 3.9 %collective-permute-start.16 = (f32[2,48,768]{2,1,0:T(8,128)S(1)}, f32[2,48,768]{2,1,0:T(8,128)S(1)}, u32[]{:S(2)}, u32[]{:S(2)}) collective-permute-start(f32[2,48,768]{2,1,0:T(8,128)S(1)} %add.95), channel_id=1, source_target_pairs={{0,14},{1,3},{2,0},{3,5},{4,2},{5,7},{6,4},{7,9},{8,6},{9,11},{10,... | collective-permute-start | bytes 884744 | tf_op jit(solution)/shard_map/ppermute | solution.py:22
  106.5 1.2 collective-permute-done.33
  107.7 5.0 %collective-permute-done.16 = f32[2,48,768]{2,1,0:T(8,128)S(1)} collective-permute-done((f32[2,48,768]{2,1,0:T(8,128)S(1)}, f32[2,48,768]{2,1,0:T(8,128)S(1)}, u32[]{:S(2)}, u32[]{:S(2)}) %collective-permute-start.16) | collective-permute-done | bytes 294944 | tf_op jit(solution)/shard_map/ppermute | solution.py:22
  112.7 1.5 %collective-permute-done.13 = f32[2,48,768]{2,1,0:T(8,128)S(1)} collective-permute-done((f32[2,48,768]{2,1,0:T(8,128)S(1)}, f32[2,48,768]{2,1,0:T(8,128)S(1)}, u32[]{:S(2)}, u32[]{:S(2)}) %collective-permute-start.13) | collective-permute-done | bytes 294944 | tf_op jit(solution)/shard_map/ppermute | solution.py:22
  114.3 1.3 %collective-permute-start.17 = (f32[48,768]{1,0:T(8,128)S(1)}, f32[48,768]{1,0:T(8,128)S(1)}, u32[]{:S(2)}, u32[]{:S(2)}) collective-permute-start(f32[48,768]{1,0:T(8,128)S(1)} %dynamic-slice_bitcast_fusion), channel_id=1, source_target_pairs={{0,16},{1,17},{2,18},{3,19},{4,20},{5,21},{6,22},{7,23},{8,24},{9,... | collective-permute-start | bytes 442376 | tf_op jit(solution)/shard_map/ppermute | solution.py:22
  116.3 3.3 %collective-permute-done.17 = f32[48,768]{1,0:T(8,128)S(1)} collective-permute-done((f32[48,768]{1,0:T(8,128)S(1)}, f32[48,768]{1,0:T(8,128)S(1)}, u32[]{:S(2)}, u32[]{:S(2)}) %collective-permute-start.17) | collective-permute-done | bytes 147488 | tf_op jit(solution)/shard_map/ppermute | solution.py:22
  (80 shorter events, 10.2 us)
Async XLA Ops:
  3.5 23.0 %collective-permute-start.1 = (f32[768,384]{1,0:T(8,128)}, f32[768,384]{1,0:T(8,128)S(1)}, u32[]{:S(2)}, u32[]{:S(2)}) collective-permute-start(f32[768,384]{1,0:T(8,128)} %bitcast.1), channel_id=1, source_target_pairs={{0,1},{1,0},{2,3},{3,2},{4,5},{5,4},{6,7},{7,6},{8,9},{9,8},{10,11... | collective-permute-start | bytes 3538952 | tf_op jit(solution)/shard_map/ppermute | solution.py:22
  3.5 6.9 %collective-permute-start.18 = (f32[3,48,256]{2,1,0:T(8,128)S(1)}, f32[3,48,256]{2,1,0:T(8,128)S(1)}, u32[]{:S(2)}, u32[]{:S(2)}) collective-permute-start(f32[3,48,256]{2,1,0:T(8,128)S(1)} %copy-done.1), channel_id=1, source_target_pairs={{0,16},{1,17},{2,18},{3,19},{4,20},{5,21},{6,22},{7,23},{8,24},{9,... | collective-permute-start | bytes 442376 | tf_op jit(solution)/shard_map/ppermute | solution.py:22
  4.5 22.0 %collective-permute-start = (f32[3,48,256]{2,1,0:T(8,128)S(1)}, f32[3,48,256]{2,1,0:T(8,128)S(1)}, u32[]{:S(2)}, u32[]{:S(2)}) collective-permute-start(f32[3,48,256]{2,1,0:T(8,128)S(1)} %copy-done.1), channel_id=1, source_target_pairs={{0,161},{1,97},{2,128},{3,224},{4,96},{5,0},{6,193},{7,33},{8,1},{... | collective-permute-start | bytes 442376 | tf_op jit(solution)/shard_map/ppermute | solution.py:22
  10.5 11.3 %collective-permute-start.19 = (f32[6,48,256]{2,1,0:T(8,128)S(1)}, f32[6,48,256]{2,1,0:T(8,128)S(1)}, u32[]{:S(2)}, u32[]{:S(2)}) collective-permute-start(f32[6,48,256]{2,1,0:T(8,128)S(1)} %pad_maximum_fusion.1.refs_8_), channel_id=1, source_target_pairs={{0,14},{1,15},{2,0},{3,1},{4,2},{5,3},{6,4},{7,5},{8,6},{9,7},{10,... | collective-permute-start | bytes 884744 | tf_op jit(solution)/shard_map/ppermute | solution.py:22
  16.2 27.3 %collective-permute-start.22 = (f32[6,48,256]{2,1,0:T(8,128)S(1)}, f32[6,48,256]{2,1,0:T(8,128)S(1)}, u32[]{:S(2)}, u32[]{:S(2)}) collective-permute-start(f32[6,48,256]{2,1,0:T(8,128)S(1)} %pad_maximum_fusion.1.refs_8_), channel_id=1, source_target_pairs={{0,2},{1,3},{2,4},{3,5},{4,6},{5,7},{6,8},{7,9},{8,10},{9,11},{10,... | collective-permute-start | bytes 884744 | tf_op jit(solution)/shard_map/ppermute | solution.py:22
  21.8 21.7 %collective-permute-start.20 = (f32[6,48,256]{2,1,0:T(8,128)S(1)}, f32[6,48,256]{2,1,0:T(8,128)S(1)}, u32[]{:S(2)}, u32[]{:S(2)}) collective-permute-start(f32[6,48,256]{2,1,0:T(8,128)S(1)} %collective-permute-done.19.refs_9_), channel_id=1, source_target_pairs={{0,14},{1,15},{2,0},{3,1},{4,2},{5,3},{6,4},{7,5},{8,6},{9,7},{10,... | collective-permute-start | bytes 884744 | tf_op jit(solution)/shard_map/ppermute | solution.py:22
  26.5 6.6 %collective-permute-start.2 = (f32[3,48,256]{2,1,0:T(8,128)S(1)}, f32[3,48,256]{2,1,0:T(8,128)S(1)}, u32[]{:S(2)}, u32[]{:S(2)}) collective-permute-start(f32[3,48,256]{2,1,0:T(8,128)S(1)} %collective-permute-done), channel_id=1, source_target_pairs={{0,32},{1,33},{2,34},{3,35},{4,36},{5,37},{6,38},{7,39},{8,40},{9,... | collective-permute-start | bytes 442376 | tf_op jit(solution)/shard_map/ppermute | solution.py:22
  33.2 15.9 %collective-permute-start.3 = (f32[6,48,256]{2,1,0:T(8,128)S(1)}, f32[6,48,256]{2,1,0:T(8,128)S(1)}, u32[]{:S(2)}, u32[]{:S(2)}) collective-permute-start(f32[6,48,256]{2,1,0:T(8,128)S(1)} %constant_dynamic-update-slice_fusion.refs_0_), channel_id=1, source_target_pairs={{0,192},{1,193},{2,194},{3,195},{4,196},{5,197},{6,198},{7,199},{8... | collective-permute-start | bytes 884744 | tf_op jit(solution)/shard_map/ppermute | solution.py:22
  43.4 7.9 %collective-permute-start.4 = (f32[6,48,256]{2,1,0:T(8,128)S(1)}, f32[6,48,256]{2,1,0:T(8,128)S(1)}, u32[]{:S(2)}, u32[]{:S(2)}) collective-permute-start(f32[6,48,256]{2,1,0:T(8,128)S(1)} %constant_dynamic-update-slice_fusion.refs_0_), channel_id=1, source_target_pairs={{0,64},{1,65},{2,66},{3,67},{4,68},{5,69},{6,70},{7,71},{8,72},{9,... | collective-permute-start | bytes 884744 | tf_op jit(solution)/shard_map/ppermute | solution.py:22
  43.4 8.3 %collective-permute-start.23 = (f32[6,48,256]{2,1,0:T(8,128)S(1)}, f32[6,48,256]{2,1,0:T(8,128)S(1)}, u32[]{:S(2)}, u32[]{:S(2)}) collective-permute-start(f32[6,48,256]{2,1,0:T(8,128)S(1)} %collective-permute-done.22.refs_15_), channel_id=1, source_target_pairs={{0,2},{1,3},{2,4},{3,5},{4,6},{5,7},{6,8},{7,9},{8,10},{9,11},{10,... | collective-permute-start | bytes 884744 | tf_op jit(solution)/shard_map/ppermute | solution.py:22
  43.4 8.8 %collective-permute-start.21 = (f32[6,48,256]{2,1,0:T(8,128)S(1)}, f32[6,48,256]{2,1,0:T(8,128)S(1)}, u32[]{:S(2)}, u32[]{:S(2)}) collective-permute-start(f32[6,48,256]{2,1,0:T(8,128)S(1)} %collective-permute-done.20.refs_10_), channel_id=1, source_target_pairs={{0,14},{1,15},{2,0},{3,1},{4,2},{5,3},{6,4},{7,5},{8,6},{9,7},{10,... | collective-permute-start | bytes 884744 | tf_op jit(solution)/shard_map/ppermute | solution.py:22
  51.4 8.0 %collective-permute-start.5 = (f32[6,48,256]{2,1,0:T(8,128)S(1)}, f32[6,48,256]{2,1,0:T(8,128)S(1)}, u32[]{:S(2)}, u32[]{:S(2)}) collective-permute-start(f32[6,48,256]{2,1,0:T(8,128)S(1)} %broadcast_select_fusion.1), channel_id=1, source_target_pairs={{0,64},{1,193},{2,66},{3,195},{4,68},{5,197},{6,70},{7,199},{8,72}... | collective-permute-start | bytes 884744 | tf_op jit(solution)/shard_map/ppermute | solution.py:22
  51.8 7.9 %collective-permute-start.24 = (f32[6,48,256]{2,1,0:T(8,128)S(1)}, f32[6,48,256]{2,1,0:T(8,128)S(1)}, u32[]{:S(2)}, u32[]{:S(2)}) collective-permute-start(f32[6,48,256]{2,1,0:T(8,128)S(1)} %collective-permute-done.23.refs_14_), channel_id=1, source_target_pairs={{0,2},{1,3},{2,4},{3,5},{4,6},{5,7},{6,8},{7,9},{8,10},{9,11},{10,... | collective-permute-start | bytes 884744 | tf_op jit(solution)/shard_map/ppermute | solution.py:22
  51.8 8.1 %collective-permute-start.6 = (f32[6,48,256]{2,1,0:T(8,128)S(1)}, f32[6,48,256]{2,1,0:T(8,128)S(1)}, u32[]{:S(2)}, u32[]{:S(2)}) collective-permute-start(f32[6,48,256]{2,1,0:T(8,128)S(1)} %constant_dynamic-update-slice_fusion.refs_0_), channel_id=1, source_target_pairs={{0,1},{1,0},{2,3},{3,2},{4,5},{5,4},{6,7},{7,6},{8,9},{9,8},{10,11... | collective-permute-start | bytes 884744 | tf_op jit(solution)/shard_map/ppermute | solution.py:22
  51.8 8.1 %collective-permute-start.7 = (f32[6,48,256]{2,1,0:T(8,128)S(1)}, f32[6,48,256]{2,1,0:T(8,128)S(1)}, u32[]{:S(2)}, u32[]{:S(2)}) collective-permute-start(f32[6,48,256]{2,1,0:T(8,128)S(1)} %collective-permute-done.3.refs_1_), channel_id=1, source_target_pairs={{0,1},{1,0},{2,3},{3,2},{4,5},{5,4},{6,7},{7,6},{8,9},{9,8},{10,11... | collective-permute-start | bytes 884744 | tf_op jit(solution)/shard_map/ppermute | solution.py:22
  52.3 7.6 %collective-permute-start.9 = (f32[6,48,256]{2,1,0:T(8,128)S(1)}, f32[6,48,256]{2,1,0:T(8,128)S(1)}, u32[]{:S(2)}, u32[]{:S(2)}) collective-permute-start(f32[6,48,256]{2,1,0:T(8,128)S(1)} %collective-permute-done.4.refs_3_), channel_id=1, source_target_pairs={{0,1},{1,0},{2,3},{3,2},{4,5},{5,4},{6,7},{7,6},{8,9},{9,8},{10,11... | collective-permute-start | bytes 884744 | tf_op jit(solution)/shard_map/ppermute | solution.py:22
  59.8 8.0 %collective-permute-start.25 = (f32[6,48,256]{2,1,0:T(8,128)S(1)}, f32[6,48,256]{2,1,0:T(8,128)S(1)}, u32[]{:S(2)}, u32[]{:S(2)}) collective-permute-start(f32[6,48,256]{2,1,0:T(8,128)S(1)} %broadcast_select_fusion), channel_id=1, source_target_pairs={{0,2},{1,15},{2,4},{3,1},{4,6},{5,3},{6,8},{7,5},{8,10},{9,7},{10,... | collective-permute-start | bytes 884744 | tf_op jit(solution)/shard_map/ppermute | solution.py:22
  70.0 11.3 %collective-permute-start.10 = (f32[2,48,768]{2,1,0:T(8,128)S(1)}, f32[2,48,768]{2,1,0:T(8,128)S(1)}, u32[]{:S(2)}, u32[]{:S(2)}) collective-permute-start(f32[2,48,768]{2,1,0:T(8,128)S(1)} %get-tuple-element.28.refs_4_), channel_id=1, source_target_pairs={{0,2},{1,15},{2,4},{3,1},{4,6},{5,3},{6,8},{7,5},{8,10},{9,7},{10,... | collective-permute-start | bytes 884744 | tf_op jit(solution)/shard_map/ppermute | solution.py:22
  72.5 15.0 %all-to-all-start = ((f32[8,3,32,128]{3,2,1,0:T(8,128)}), f32[8,3,32,128]{3,2,1,0:T(8,128)S(1)}, u32[]{:S(2)}, u32[]{:S(2)}) async-start(f32[8,3,32,128]{3,2,1,0:T(8,128)} %add.103), calls=%async_computation | async-start | bytes 786432 | tf_op jit(solution)/shard_map/all_to_all | solution.py:292
  79.7 11.4 %collective-permute-start.14 = (f32[2,48,768]{2,1,0:T(8,128)S(1)}, f32[2,48,768]{2,1,0:T(8,128)S(1)}, u32[]{:S(2)}, u32[]{:S(2)}) collective-permute-start(f32[2,48,768]{2,1,0:T(8,128)S(1)} %get-tuple-element.31.refs_5_), channel_id=1, source_target_pairs={{0,14},{1,3},{2,0},{3,5},{4,2},{5,7},{6,4},{7,9},{8,6},{9,11},{10,... | collective-permute-start | bytes 884744 | tf_op jit(solution)/shard_map/ppermute | solution.py:22
  81.3 11.1 %collective-permute-start.11 = (f32[2,48,768]{2,1,0:T(8,128)S(1)}, f32[2,48,768]{2,1,0:T(8,128)S(1)}, u32[]{:S(2)}, u32[]{:S(2)}) collective-permute-start(f32[2,48,768]{2,1,0:T(8,128)S(1)} %add.90), channel_id=1, source_target_pairs={{0,2},{1,15},{2,4},{3,1},{4,6},{5,3},{6,8},{7,5},{8,10},{9,7},{10,... | collective-permute-start | bytes 884744 | tf_op jit(solution)/shard_map/ppermute | solution.py:22
  87.5 5.8 %collective-permute-start.27 = (f32[3,32,128]{2,1,0:T(8,128)S(1)}, f32[3,32,128]{2,1,0:T(8,128)S(1)}, u32[]{:S(2)}, u32[]{:S(2)}) collective-permute-start(f32[3,32,128]{2,1,0:T(8,128)S(1)} %reduce_sum.9), channel_id=1, source_target_pairs={{0,2},{1,15},{2,0},{3,5},{4,6},{5,3},{6,4},{7,9},{8,10},{9,7},{10,... | collective-permute-start | bytes 147464 | tf_op jit(solution)/shard_map/ppermute | solution.py:22
  87.6 5.7 %collective-permute-start.28 = (f32[3,32,128]{2,1,0:T(8,128)S(1)}, f32[3,32,128]{2,1,0:T(8,128)S(1)}, u32[]{:S(2)}, u32[]{:S(2)}) collective-permute-start(f32[3,32,128]{2,1,0:T(8,128)S(1)} %reduce_sum.9), channel_id=1, source_target_pairs={{0,16},{1,17},{2,18},{3,19},{4,20},{5,21},{6,22},{7,23},{8,24},{9,... | collective-permute-start | bytes 147464 | tf_op jit(solution)/shard_map/ppermute | solution.py:22
  88.9 5.1 %collective-permute-start.29 = (f32[3,32,128]{2,1,0:T(8,128)S(1)}, f32[3,32,128]{2,1,0:T(8,128)S(1)}, u32[]{:S(2)}, u32[]{:S(2)}) collective-permute-start(f32[3,32,128]{2,1,0:T(8,128)S(1)} %reduce_sum.9), channel_id=1, source_target_pairs={{0,18},{1,31},{2,16},{3,21},{4,22},{5,19},{6,20},{7,25},{8,26},{9,... | collective-permute-start | bytes 147464 | tf_op jit(solution)/shard_map/ppermute | solution.py:22
  91.1 11.1 %collective-permute-start.15 = (f32[2,48,768]{2,1,0:T(8,128)S(1)}, f32[2,48,768]{2,1,0:T(8,128)S(1)}, u32[]{:S(2)}, u32[]{:S(2)}) collective-permute-start(f32[2,48,768]{2,1,0:T(8,128)S(1)} %add.94), channel_id=1, source_target_pairs={{0,14},{1,3},{2,0},{3,5},{4,2},{5,7},{6,4},{7,9},{8,6},{9,11},{10,... | collective-permute-start | bytes 884744 | tf_op jit(solution)/shard_map/ppermute | solution.py:22
  92.5 13.7 %collective-permute-start.12 = (f32[2,48,768]{2,1,0:T(8,128)S(1)}, f32[2,48,768]{2,1,0:T(8,128)S(1)}, u32[]{:S(2)}, u32[]{:S(2)}) collective-permute-start(f32[2,48,768]{2,1,0:T(8,128)S(1)} %add.91), channel_id=1, source_target_pairs={{0,2},{1,15},{2,4},{3,1},{4,6},{5,3},{6,8},{7,5},{8,10},{9,7},{10,... | collective-permute-start | bytes 884744 | tf_op jit(solution)/shard_map/ppermute | solution.py:22
  94.0 12.3 %collective-permute-start.30 = (f32[3,32,128]{2,1,0:T(8,128)S(1)}, f32[3,32,128]{2,1,0:T(8,128)S(1)}, u32[]{:S(2)}, u32[]{:S(2)}) collective-permute-start(f32[3,32,128]{2,1,0:T(8,128)S(1)} %add_add_fusion.2), channel_id=1, source_target_pairs={{0,8},{1,9},{2,10},{3,11},{4,12},{5,13},{6,14},{7,15},{8,0},{9,1},... | collective-permute-start | bytes 147464 | tf_op jit(solution)/shard_map/ppermute | solution.py:22
  97.3 9.0 %collective-permute-start.31 = (f32[3,32,128]{2,1,0:T(8,128)S(1)}, f32[3,32,128]{2,1,0:T(8,128)S(1)}, u32[]{:S(2)}, u32[]{:S(2)}) collective-permute-start(f32[3,32,128]{2,1,0:T(8,128)S(1)} %add_add_fusion.2), channel_id=1, source_target_pairs={{0,4},{1,5},{2,6},{3,7},{4,8},{5,9},{6,10},{7,11},{8,12},{9,13},{1... | collective-permute-start | bytes 147464 | tf_op jit(solution)/shard_map/ppermute | solution.py:22
  98.6 7.8 %collective-permute-start.32 = (f32[3,32,128]{2,1,0:T(8,128)S(1)}, f32[3,32,128]{2,1,0:T(8,128)S(1)}, u32[]{:S(2)}, u32[]{:S(2)}) collective-permute-start(f32[3,32,128]{2,1,0:T(8,128)S(1)} %add_add_fusion.2), channel_id=1, source_target_pairs={{0,12},{1,13},{2,14},{3,15},{4,0},{5,1},{6,2},{7,3},{8,4},{9,5},{1... | collective-permute-start | bytes 147464 | tf_op jit(solution)/shard_map/ppermute | solution.py:22
  102.3 10.5 %collective-permute-start.16 = (f32[2,48,768]{2,1,0:T(8,128)S(1)}, f32[2,48,768]{2,1,0:T(8,128)S(1)}, u32[]{:S(2)}, u32[]{:S(2)}) collective-permute-start(f32[2,48,768]{2,1,0:T(8,128)S(1)} %add.95), channel_id=1, source_target_pairs={{0,14},{1,3},{2,0},{3,5},{4,2},{5,7},{6,4},{7,9},{8,6},{9,11},{10,... | collective-permute-start | bytes 884744 | tf_op jit(solution)/shard_map/ppermute | solution.py:22
  106.2 8.0 %collective-permute-start.13 = (f32[2,48,768]{2,1,0:T(8,128)S(1)}, f32[2,48,768]{2,1,0:T(8,128)S(1)}, u32[]{:S(2)}, u32[]{:S(2)}) collective-permute-start(f32[2,48,768]{2,1,0:T(8,128)S(1)} %add.92), channel_id=1, source_target_pairs={{0,2},{1,15},{2,4},{3,1},{4,6},{5,3},{6,8},{7,5},{8,10},{9,7},{10,... | collective-permute-start | bytes 884744 | tf_op jit(solution)/shard_map/ppermute | solution.py:22
  114.3 5.2 %collective-permute-start.17 = (f32[48,768]{1,0:T(8,128)S(1)}, f32[48,768]{1,0:T(8,128)S(1)}, u32[]{:S(2)}, u32[]{:S(2)}) collective-permute-start(f32[48,768]{1,0:T(8,128)S(1)} %dynamic-slice_bitcast_fusion), channel_id=1, source_target_pairs={{0,16},{1,17},{2,18},{3,19},{4,20},{5,21},{6,22},{7,23},{8,24},{9,... | collective-permute-start | bytes 442376 | tf_op jit(solution)/shard_map/ppermute | solution.py:22
  (8 other events, 72.9 us)
